TPU v7x, 512 devices: a whole 4x8x8 slice. The times are simulated.
512 devices in a mesh: wide: 128 (over y, z, core), pair: 4 (over x).
Axes of the slice: x: 4, y: 8, z: 8, core: 2. Of those that a mesh axis runs over, the one named last changes fastest.
Arguments:
- blocks: bfloat16 [2048, 1024, 512], P('pair', 'wide'), may hold values from -6 to 6
- basis_a: bfloat16 [1024, 64], replicated, may hold values from -0.1875 to 0.1875
- basis_b: bfloat16 [512, 64], replicated, may hold values from -0.25 to 0.25
- sketch: bfloat16 [2048, 64], P(('pair', 'wide')), may hold values from -6 to 6
Outputs:
- transfer: float32 [4096, 64], P(('wide', 'pair'))
- coefficients: float32 [2048, 64], P(('pair', 'wide'))
All inputs are finite; a program needn't handle non-finite values.
Results may differ from a plain program's by a relative error of at most 0.0041.
Values may be sent and summed in bfloat16 or wider, within the bound.
A program may use at most 64 MiB of HBM per device.

v0:
```python
import jax
import jax.numpy as jnp
from jax import lax
from jax.sharding import PartitionSpec as P


def orthonormal(sketched, gram):
    lower = jnp.linalg.cholesky(gram)
    return lax.linalg.triangular_solve(
        lower, sketched, left_side=False, lower=True, transpose_a=True
    )


def per_device(blocks, basis_a, basis_b, sketch):
    fibres = sketch.shape[0]
    rank_a = basis_a.shape[1]
    rank_b = basis_b.shape[1]
    narrowed = jnp.einsum(
        "fac,cr->far", blocks, basis_b, preferred_element_type=jnp.float32
    ).astype(jnp.bfloat16)
    regrouped = lax.all_to_all(narrowed, "wide", split_axis=0, concat_axis=1, tiled=True)
    projected = jnp.einsum(
        "ap,far->fpr", basis_a, regrouped, preferred_element_type=jnp.float32
    ).astype(jnp.bfloat16)
    projected = projected.reshape(fibres, rank_a * rank_b)
    partial_value = jnp.einsum("fj,fk->jk", projected, sketch, preferred_element_type=jnp.float32)
    own_count = rank_a * rank_b // lax.axis_size(("wide", "pair"))
    sketch_all = lax.psum(partial_value, ("wide", "pair"))
    gram_matrix = jnp.dot(sketch_all.T, sketch_all, precision=lax.Precision.HIGHEST)
    parent_basis = orthonormal(sketch_all, gram_matrix)
    first_row = lax.axis_index(("wide", "pair")) * own_count
    own_basis = lax.dynamic_slice_in_dim(parent_basis, first_row, own_count, 0)
    transfer = own_basis * jnp.sqrt(jnp.float32(rank_a * rank_b))
    coefficients = jnp.dot(
        projected.astype(jnp.float32), parent_basis, precision=lax.Precision.HIGHEST
    )
    return (transfer, coefficients)


def solution(mesh):
    placed = (P("pair", "wide", None), P(), P(), P(("pair", "wide"), None))
    return jax.shard_map(
        per_device,
        mesh=mesh,
        in_specs=placed,
        out_specs=(P(("wide", "pair"), None), P(("pair", "wide"), None)),
        check_vma=False,
    )
```

profile of v0, /device:TPU:1, one launch (start us, length us, event | category | flops | bytes accessed | tf_op | source)
XLA Modules:
  0.0 346.7 jit_solution(4763148819996868437)
XLA Ops:
  7.2 0.0 copy-start
  7.2 0.0 all-reduce.2.cloned.1.call-start
  7.2 3.4 convolution_convert_fusion
  10.7 0.0 copy-start.1
  10.7 0.6 reshape.19
  11.3 37.6 %all_to_all.18 = bf16[128,2,1024]{2,1,0:T(2,128)(2,1)S(1)} all-to-all(bf16[128,2,1024]{2,1,0:T(2,128)(2,1)S(1)} %reshape.19), channel_id=1, replica_groups=mesh['wide'=128,'pair'=4] {'wide'}, dimensions={0} | all-to-all | bytes 1048576 | tf_op jit(solution)/shard_map/all_to_all | solution.py:21
  48.9 0.6 reshape.20
  49.5 0.0 copy-done
  49.5 0.5 fusion
  50.0 0.1 copy.19
  50.1 0.1 reshape.16
  50.3 1.4 fusion.9
  51.7 0.0 all-reduce.2.cloned.1.call-update
  51.7 269.2 %all-reduce.2.cloned.1.call-done = f32[4096,64]{0,1:T(8,128)} async-done(((f32[4096,64]{0,1:T(8,128)}), f32[4096,64]{0,1:T(8,128)}) %all-reduce.2.cloned.1.call-update) | async-done | bytes 1048592 | tf_op jit(solution)/shard_map/psum | solution.py:28
  320.9 2.5 fusion.10
  323.4 0.1 copy.20
  323.5 5.8 %cholesky.16 = f32[64,64]{1,0:T(8,128)S(1)} custom-call(f32[64,64]{1,0:T(8,128)S(1)} %fusion.8), custom_call_target="Cholesky" | custom-call | tf_op jit(solution)/shard_map/jit(cholesky)/cholesky | solution.py:8
  329.4 0.6 compare_reduce_fusion
  330.1 0.7 fusion.5
  330.7 4.9 %custom-call.6 = f32[1,64,64]{1,2,0:T(8,128)S(1)} custom-call(f32[1,64,64]{2,1,0:T(8,128)S(1)} %fusion.5), custom_call_target="InvertDiagBlocksLowerTriangular" | custom-call | tf_op jit(solution)/shard_map/triangular_solve | solution.py:9
  335.6 2.3 fusion.6
  337.9 1.2 fusion.11
  339.1 0.1 dynamic-slice_multiply_fusion
  339.2 0.7 copy.21
  (3 shorter events, 0.0 us)
Async XLA Ops:
  7.2 42.4 %copy-start = (bf16[1024,64]{0,1:T(8,128)(2,1)S(1)}, bf16[1024,64]{0,1:T(8,128)(2,1)}, u32[]{:S(2)}) copy-start(bf16[1024,64]{0,1:T(8,128)(2,1)} %param.5) | copy-start | bytes 393220
  7.2 313.7 %all-reduce.2.cloned.1.call-start = ((), (), s32[]{:S(2)}) async-start(), calls=%async_computation.1 | async-start | bytes 2097152 | tf_op jit(solution)/shard_map/psum | solution.py:28
  10.7 39.6 %copy-start.1 = (bf16[4,64]{1,0:T(4,128)(2,1)S(1)}, bf16[4,64]{1,0:T(4,128)(2,1)}, u32[]{:S(2)}) copy-start(bf16[4,64]{1,0:T(4,128)(2,1)} %param.7) | copy-start | bytes 1540
Sparse Core Ops, SparseCore 0:
  51.8 269.0 all-reduce.1
where the time goes:
time: 347 us
  waiting for transfers between devices  269 us (78%)
  blocking collectives  37.6 us (11%)
  between operations  14.1 us (4%)
  other arithmetic  12.2 us (4%)
  matrix products  11.3 us (3%)
    psum x1, waiting for transfers between devices, per_device(): sketch_all = lax.psum(partial_value, ('wide', 'pair'))  269 us
    all_to_all x1, blocking collectives, per_device(): lax.all_to_all(narrowed, 'wide', split_axis=0, concat_axis=1, tiled=True)  37.6 us
  transfers between devices with their start and end apart: 1, of which 1 were waited for; matrix products, arithmetic and copies ran while one was open for 0% of the time, Pallas kernels for 0%

commit v1 on v0

v1 whole, which is shorter than its diff:
```python
import functools

import jax
import jax.numpy as jnp
from jax import lax
from jax.experimental import pallas as pl
from jax.experimental.pallas import tpu as pltpu
from jax.sharding import PartitionSpec as P

MESH = pl.DeviceIdType.MESH
F32 = jnp.float32
BF16 = jnp.bfloat16
CONTRACT_LAST = (((1,), (1,)), ((), ()))
CONTRACT_FIRST = (((0,), (0,)), ((), ()))


def iota(shape, dim):
    return lax.broadcasted_iota(jnp.int32, shape, dim)


def dot(a, b, dims=(((1,), (0,)), ((), ())), precision=None):
    return lax.dot_general(a, b, dims, preferred_element_type=F32, precision=precision)


def low_half(shape):
    return iota(shape, 1) < 64


def swap_halves(v):
    return pltpu.roll(v, 64, 1)


def one_hot(mask):
    return jnp.where(mask, 1.0, 0.0).astype(BF16)


def kernel(sizes, blocks, basis_bt, basis_at, sketch, transfer, coefficients, *scratch):
    X, Y, Z = sizes
    ZC = Z * 2
    YL = max(Y // 2, 1)
    chips = Y * Z
    FX = chips * 8
    FC = FX // 8
    (block_in, wide_n, packed, packed_in, s_own, s_zc, s_y, s_all, t_out, t_in, sp_out, sp_in, z_out, z_in,
     mz, s_full, m_to, m_from, w_rows, gram_out, gram_in, y_out, y_in, y2_out, y2_in, x_mat,
     in_sem, s_a, r_a, s_b, r_b, s_p, r_p, s_t, r_t, s_z1, r_z1, s_y1, r_y1, s_z2, r_z2, s_x1, r_x1,
     s_g, r_g, s_yz, r_yz, s_yy, r_yy) = scratch

    wide = lax.axis_index("wide")
    x = lax.axis_index("pair")
    core = wide % 2
    chip = wide // 2
    z = chip % Z
    y = chip // Z

    def at(dx=0, dy=0, dz=0, dc=0):
        row = ((y + dy) % Y) * Z + (z + dz) % Z
        return (row * 2 + (core + dc) % 2, (x + dx) % X)

    waits = []

    def send(src, dst, ssem, rsem, peer):
        copy = pltpu.make_async_remote_copy(
            src_ref=src, dst_ref=dst, send_sem=ssem, recv_sem=rsem, device_id=peer, device_id_type=MESH
        )
        copy.start()
        waits.append(copy)
        return copy

    def receive(copies):
        for copy in copies:
            copy.wait_recv()

    zc_peers = [(dc, dz) for dc in range(2) for dz in range(Z) if dc or dz]
    yc_peers = [(dc, dy) for dc in range(2) for dy in range(Y) if dc or dy]
    xc_peers = [(dc, dx) for dc in range(2) for dx in range(X) if dc or dx]

    loads = [
        pltpu.make_async_copy(blocks.at[pl.ds(i * FX, FX)], block_in.at[i], in_sem.at[i]) for i in range(8)
    ]
    for load in loads:
        load.start()

    barrier = pltpu.get_barrier_semaphore()
    met = 0
    for dc, dz in zc_peers:
        pl.semaphore_signal(barrier, inc=1, device_id=at(dz=dz, dc=dc), device_id_type=MESH)
        met += 1
    for dc, dy in yc_peers:
        if dy:
            pl.semaphore_signal(barrier, inc=1, device_id=at(dy=dy, dc=dc), device_id_type=MESH)
            met += 1
    for dc, dx in xc_peers:
        if dx:
            pl.semaphore_signal(barrier, inc=1, device_id=at(dx=dx, dc=dc), device_id_type=MESH)
            met += 1

    twice = one_hot(iota((64, 128), 1) % 64 == iota((64, 128), 0))
    s_mine = dot(sketch[...], twice)
    s_own[...] = s_mine
    zc = z * 2 + core
    s_zc[zc] = s_mine
    pl.semaphore_wait(barrier, met)

    got_a = [
        send(s_own, s_zc.at[zc], s_a.at[dc, dz], r_a.at[dc, dz], at(dz=dz, dc=dc)) for dc, dz in zc_peers
    ]

    basis2 = jnp.concatenate([basis_bt[...], basis_bt[...]], axis=0)

    def narrow(i, carry):
        pltpu.make_async_copy(blocks.at[pl.ds(i * FX, FX)], block_in.at[i], in_sem.at[i]).wait()
        wide_n[...] = dot(block_in[i], basis2, CONTRACT_LAST)
        rows = pl.ds(pl.multiple_of(i * FC, FC), FC)
        low = low_half((FC, 128))
        odd = (iota((FC, 128), 1) // 32) % 2 == 1
        for t in range(2):
            part = [wide_n[pl.ds(t * 4 + q, FC, stride=8), :] for q in range(4)]
            first = jnp.where(low, part[0], part[2])
            second = jnp.where(low, part[1], part[3])
            lanes = slice(t * 128, t * 128 + 128)
            packed[0, rows, lanes] = jnp.where(odd, pltpu.roll(second, 32, 1), first).astype(BF16)
            packed[1, rows, lanes] = jnp.where(odd, second, pltpu.roll(first, 96, 1)).astype(BF16)
        return carry

    lax.fori_loop(0, 4, narrow, 0)

    receive(got_a)
    half = ZC // 2
    lo = jnp.concatenate([s_zc[i] for i in range(half)], axis=0)
    hi = jnp.concatenate([s_zc[half + i] for i in range(half)], axis=0)
    rows_h = half * 4
    s_y[y] = jnp.where(low_half((rows_h, 128)), lo, hi).astype(BF16)
    got_b = [send(s_y.at[y], s_y.at[y], s_b.at[dy], r_b.at[dy], at(dy=dy)) for dy in range(1, Y)]

    lax.fori_loop(4, 8, narrow, 0)
    partner = at(dc=1)
    got_p = send(packed.at[1 - core], packed_in, s_p, r_p, partner)

    AB = min(chips * 16, 128)
    base = pl.multiple_of((chip * 16 // AB) * AB, AB)
    a_part = basis_at[:, pl.ds(base, AB)]
    MR = chips * 4

    def chip_of(index):
        zy = index // 4
        return (zy % Y) * Z + zy // Y

    col = iota((AB, 256), 1)
    pick = base + iota((AB, 256), 0) == (
        chip * 16 + ((core + (col // 32) % 2) % 2) * 8 + ((col // 8) % 4) * 2 + (col // 64) % 2
    )
    a_cols = dot(a_part, one_hot(pick)).astype(BF16)
    spread = one_hot(chip_of(iota((MR, chips), 0)) == iota((MR, chips), 1))
    rows_a = dot(spread, a_cols)
    for rh in range(2):
        keep = iota((MR, 256), 1) % 8 == rh * 4 + iota((MR, 256), 0) % 4
        m_to[rh] = jnp.where(keep, rows_a, 0.0).astype(BF16)
    row = iota((128, AB), 0)
    pick = base + iota((128, AB), 1) == chip * 16 + ((core + row // 64) % 2) * 8 + (row // 8) % 8
    a_rows = dot(one_hot(pick), a_part, CONTRACT_LAST).astype(BF16)
    spread = one_hot(chip_of(iota((chips, MR), 1)) == iota((chips, MR), 0))
    cols_a = dot(a_rows, spread)
    for rh in range(2):
        keep = iota((128, MR), 0) % 8 == rh * 4 + iota((128, MR), 1) % 4
        m_from[:, rh * MR : (rh + 1) * MR] = jnp.where(keep, cols_a, 0.0).astype(BF16)

    receive(got_b)
    low = low_half((rows_h, 128))
    for i in range(Y):
        v = s_y[i].astype(F32)
        w = swap_halves(v)
        s_all[2 * i * rows_h : (2 * i + 1) * rows_h, :] = jnp.where(low, v, w).astype(BF16)
        s_all[(2 * i + 1) * rows_h : (2 * i + 2) * rows_h, :] = jnp.where(low, w, v).astype(BF16)

    low = low_half((32, 128))
    for cc in range(2):
        t = dot(packed[cc], s_all[...], CONTRACT_FIRST)
        for ah in range(4):
            pair = jnp.where(low, t[ah * 64 : ah * 64 + 32], t[ah * 64 + 32 : ah * 64 + 64])
            for xx in range(4):
                t_out[cc, xx, ah] = pair[xx * 8 : xx * 8 + 8]
    got_t = [
        send(
            t_out.at[(core + dc) % 2, (x + dx) % X],
            t_in.at[dc, dx],
            s_t.at[dc, dx],
            r_t.at[dc, dx],
            at(dx=dx, dc=dc),
        )
        for dc, dx in xc_peers
    ]
    mine = t_out[core, x]
    receive(got_t)
    for dx in range(1, X):
        mine = mine + t_in[0, dx]
    other = t_in[1, 0]
    for dx in range(1, X):
        other = other + t_in[1, dx]
    u = jnp.concatenate([mine.reshape(32, 128), other.reshape(32, 128)], axis=0)
    low = low_half((64, 128))
    v = swap_halves(u)
    u = jnp.concatenate([jnp.where(low, u, v), jnp.where(low, v, u)], axis=0)
    top = u.astype(BF16)
    rest = (u - top.astype(F32)).astype(BF16)
    u = jnp.concatenate([top, rest], axis=0)
    low = low_half((MR, 128))
    part = jnp.where(low, dot(m_to[0], u), dot(m_to[1], u))
    RZ = Y * 4
    for i in range(Z):
        sp_out[i] = part[i * RZ : (i + 1) * RZ].astype(BF16)

    got = [
        send(sp_out.at[(z + dz) % Z], sp_in.at[dz], s_z1.at[dz], r_z1.at[dz], at(dz=dz)) for dz in range(1, Z)
    ]
    total = sp_out[z].astype(F32)
    receive(got)
    for dz in range(1, Z):
        total = total + sp_in[dz].astype(F32)
    z_out[...] = total.astype(BF16)
    got = [send(z_out, z_in.at[dy], s_y1.at[dy], r_y1.at[dy], at(dy=dy)) for dy in range(1, Y)]
    receive(got)
    for dy in range(1, Y):
        total = total + z_in[dy].astype(F32)
    for i in range(Y):
        mz[i] = total[i * 4 : i * 4 + 4]
    s_full[x, z] = total.astype(BF16)
    spot = s_full.at[x, z]
    got = [send(spot, spot, s_z2.at[dz], r_z2.at[dz], at(dz=dz)) for dz in range(1, Z)]
    receive(got)
    spot = s_full.at[x]
    got = [send(spot, spot, s_x1.at[dx], r_x1.at[dx], at(dx=dx)) for dx in range(1, X)]
    receive(got)

    s_x = [s_full[i].reshape(MR, 128) for i in range(X)]
    big = dot(s_x[0], s_x[0], CONTRACT_FIRST)
    for i in range(1, X):
        big = big + dot(s_x[i], s_x[i], CONTRACT_FIRST)
    gram_out[...] = swap_halves(big[0:64]) + big[64:128]
    got_g = send(gram_out, gram_in, s_g, r_g, partner)

    low = low_half((MR, 128))
    rhs = []
    for xp in range(X // 2):
        s0 = s_x[2 * xp].astype(F32)
        s1 = s_x[2 * xp + 1].astype(F32)
        rhs.append(
            jnp.concatenate(
                [jnp.where(low, s0, swap_halves(s1)), jnp.where(low, swap_halves(s0), s1)], axis=0
            ).astype(BF16)
        )
    low = low_half((128, 128))
    for xp in range(X // 2):
        w = dot(m_from[...], rhs[xp])
        v = swap_halves(w)
        even = jnp.where(low, w, v)
        odd = jnp.where(low, v, w)
        for a in range(16):
            w_rows[a, 2 * xp] = even[a * 8 : a * 8 + 8]
            w_rows[a, 2 * xp + 1] = odd[a * 8 : a * 8 + 8]
    receive([got_p])
    w0 = w_rows[0:8].reshape(256, 128).astype(BF16)
    w1 = w_rows[8:16].reshape(256, 128).astype(BF16)
    ylow = dot(packed[core, 0 : FX // 2, :], w0) + dot(packed_in[0 : FX // 2, :], w1)
    yhigh = dot(packed[core, FX // 2 : FX, :], w0) + dot(packed_in[FX // 2 : FX, :], w1)
    ypart = jnp.where(low_half((FX // 2, 128)), ylow, yhigh)
    for i in range(YL):
        for j in range(Z):
            y_out[j, i] = ypart[(i * Z + j) * 8 : (i * Z + j) * 8 + 8]
    got_y = [
        send(y_out.at[(z + dz) % Z], y_in.at[dz], s_yz.at[dz], r_yz.at[dz], at(dz=dz)) for dz in range(1, Z)
    ]

    receive([got_g])
    g = gram_out[...] + gram_in[...]
    low = low_half((64, 128))
    g = jnp.where(low, jnp.where(iota((64, 128), 0) == iota((64, 128), 1), 1.0, 0.0), g)
    tiles = [g[i * 8 : i * 8 + 8] for i in range(8)]
    sub = iota((8, 128), 0)

    def eliminate(tiles, first, last):
        for j in range(first, last):
            pos = j % 8
            line = tiles[j // 8][pos : pos + 1]
            line_scaled = line / line[:, 64 + j : 65 + j]
            for i in range(j // 8, 8):
                c = tiles[i][:, 64 + j : 65 + j]
                if i == j // 8:
                    c = jnp.where(sub[:, 0:1] > pos, c, 0.0)
                tiles[i] = tiles[i] - c * line_scaled
        return tiles

    tiles = eliminate(tiles, 0, 24)

    receive(got_y)
    acc = y_out[z]
    for dz in range(1, Z):
        acc = acc + y_in[dz]
    for i in range(YL):
        for cc in range(2):
            y2_out[i, cc] = acc[i, cc * 4 : cc * 4 + 4]
    got_y = [
        send(
            y2_out.at[((y + dy) % Y) % YL, (core + dc) % 2],
            y2_in.at[dc, dy],
            s_yy.at[dc, dy],
            r_yy.at[dc, dy],
            at(dy=dy, dc=dc),
        )
        for dc, dy in yc_peers
    ]
    tiles = eliminate(tiles, 24, 64)
    x_mat[...] = jnp.concatenate(tiles, axis=0)
    elim = x_mat[...]
    diagonal = jnp.where(iota((64, 128), 1) == iota((64, 128), 0) + 64, elim, 0.0)
    pivots = jnp.sum(diagonal, axis=1, keepdims=True)
    inverse = elim[:, 0:64] * (1.0 / jnp.sqrt(pivots))

    receive(got_y)
    acc = y2_out[y % YL, core]
    for dc, dy in yc_peers:
        acc = acc + y2_in[dc, dy]
    acc = jnp.where(y // YL == 0, acc, swap_halves(acc)) if Y > 1 else acc
    s_mine = mz[y]
    rows = jnp.concatenate([s_mine, swap_halves(s_mine), acc, acc], axis=0)
    out = dot(rows[:, 0:64], inverse, CONTRACT_LAST, lax.Precision.HIGHEST)
    transfer[...] = out[0:8] * float((chips * 64) ** 0.5)
    coefficients[...] = out[8:12]

    for copy in waits:
        copy.wait_send()


def scratch_for(sizes, cb):
    X, Y, Z = sizes
    ZC = Z * 2
    YL = max(Y // 2, 1)
    chips = Y * Z
    FX = chips * 8
    MR = chips * 4
    RZ = Y * 4
    dma = pltpu.SemaphoreType.DMA
    return [
        pltpu.VMEM((8, FX, cb), BF16),
        pltpu.VMEM((FX, 128), F32),
        pltpu.VMEM((2, FX, 256), BF16),
        pltpu.VMEM((FX, 256), BF16),
        pltpu.VMEM((4, 128), F32),
        pltpu.VMEM((ZC, 4, 128), F32),
        pltpu.VMEM((Y, ZC * 2, 128), BF16),
        pltpu.VMEM((FX, 128), BF16),
        pltpu.VMEM((2, 4, 4, 8, 128), F32),
        pltpu.VMEM((2, X, 4, 8, 128), F32),
        pltpu.VMEM((Z, RZ, 128), BF16),
        pltpu.VMEM((Z, RZ, 128), BF16),
        pltpu.VMEM((RZ, 128), BF16),
        pltpu.VMEM((Y, RZ, 128), BF16),
        pltpu.VMEM((Y, 4, 128), F32),
        pltpu.VMEM((X, Z, RZ, 128), BF16),
        pltpu.VMEM((2, MR, 256), BF16),
        pltpu.VMEM((128, 2 * MR), BF16),
        pltpu.VMEM((16, 4, 8, 128), F32),
        pltpu.VMEM((64, 128), F32),
        pltpu.VMEM((64, 128), F32),
        pltpu.VMEM((Z, YL, 8, 128), F32),
        pltpu.VMEM((Z, YL, 8, 128), F32),
        pltpu.VMEM((YL, 2, 4, 128), F32),
        pltpu.VMEM((2, Y, 4, 128), F32),
        pltpu.VMEM((64, 128), F32),
        dma((8,)),
        dma((2, Z)), dma((2, Z)),
        dma((Y,)), dma((Y,)),
        dma, dma,
        dma((2, X)), dma((2, X)),
        dma((Z,)), dma((Z,)),
        dma((Y,)), dma((Y,)),
        dma((Z,)), dma((Z,)),
        dma((X,)), dma((X,)),
        dma, dma,
        dma((Z,)), dma((Z,)),
        dma((2, Y)), dma((2, Y)),
    ]


def per_device(sizes, blocks, basis_a, basis_b, sketch):
    fibres, own_a, cb = blocks.shape
    vmem = pl.BlockSpec(memory_space=pltpu.VMEM)
    return pl.pallas_call(
        functools.partial(kernel, sizes),
        out_shape=(jax.ShapeDtypeStruct((8, 64), F32), jax.ShapeDtypeStruct((4, 64), F32)),
        in_specs=[pl.BlockSpec(memory_space=pl.ANY), vmem, vmem, vmem],
        out_specs=(vmem, vmem),
        scratch_shapes=scratch_for(sizes, cb),
        compiler_params=pltpu.CompilerParams(collective_id=0, has_side_effects=True),
        name="tucker",
    )(blocks.reshape(fibres * own_a, cb), basis_b.T, basis_a.T, sketch)


def solution(mesh):
    chips = mesh.shape["wide"] // 2
    side = int(round(chips ** 0.5))
    sizes = (mesh.shape["pair"], side, chips // side)
    placed = (P("pair", "wide", None), P(), P(), P(("pair", "wide"), None))
    return jax.shard_map(
        functools.partial(per_device, sizes),
        mesh=mesh,
        in_specs=placed,
        out_specs=(P(("wide", "pair"), None), P(("pair", "wide"), None)),
        check_vma=False,
    )
```

time: 347 us -> 69.8 us (0.20)
  waiting for transfers between devices: 269 us -> 0 us
  Pallas kernels: 0 us -> 66.5 us
  blocking collectives: 37.6 us -> 0 us
  between operations: 14.1 us -> 0.64 us
  other arithmetic: 12.2 us -> 0 us
  matrix products: 11.3 us -> 0 us
    psum x1 -> x0, waiting for transfers between devices: 269 us -> none  [per_device(): sketch_all = lax.psum(partial_value, ('wide', 'pair'))]
    pallas_call x0 -> x1, Pallas kernels: none -> 66.5 us  [per_device(): pl.pallas_call(functools.partial(kernel, sizes), out_shape=(jax.ShapeDtyp...]
    all_to_all x1 -> x0, blocking collectives: 37.6 us -> none  [per_device(): lax.all_to_all(narrowed, 'wide', split_axis=0, concat_axis=1, tiled=True)]
    another operation x5 -> x0, other arithmetic: 12.1 us -> none  [the longest x3 6.52 us: orthonormal(): lower = jnp.linalg.cholesky(gram)]
    dot_general x5 -> x0, matrix products: 9.02 us -> none  [the longest x1 3.45 us: per_device(): jnp.einsum('fac,cr->far', blocks, basis_b, preferred_element_type=jnp.flo...]
  transfers between devices with their start and end apart: 1 -> 0, of which waited for: 1 -> 0; matrix products, arithmetic and copies ran while one was open for 0% -> 0% of each run, Pallas kernels for 0% -> 0%
where the time goes in v1:
time: 69.8 us; the launch traced here: 69.7 us
  Pallas kernels  66.5 us (95%)
  local copies, waits for them, and re-layouts  2.5 us (4%)
    pallas_call x1, Pallas kernels, per_device(): pl.pallas_call(functools.partial(kernel, sizes), out_shape=(jax.ShapeDtyp...  66.5 us
    unnamed x2, local copies, waits for them, and re-layouts  2.5 us

profile of v1, /device:TPU:1, one launch (start us, length us, event | category | flops | bytes accessed | tf_op | source)
XLA Modules:
  0.0 69.7 jit_solution(17959577506498967352)
XLA Ops:
  0.6 66.5 %tucker.1 = (f32[8,64]{1,0:T(8,128)}, f32[4,64]{1,0:T(4,128)}) custom-call(bf16[4096,512]{1,0:T(8,128)(2,1)} %bitcast.3, bf16[64,512]{1,0:T(8,128)(2,1)} %bitcast.5, bf16[64,1024]{1,0:T(8,128)(2,1)} %bitcast.4, bf16[4,64]{1,0:T(4,128)(2,1)} %sketch.1), custom_call_target="tpu_custom_call" | custom-call | tf_op jit(solution)/shard_map/tucker/pallas_call | solution.py:388
  67.2 1.3 %copy.8 = f32[8,64]{1,0:T(8,128)} copy(f32[8,64]{1,0:T(8,128)} %get-tuple-element.4) | data formatting | bytes 4096
  68.4 1.2 %copy.9 = f32[4,64]{1,0:T(4,128)} copy(f32[4,64]{1,0:T(4,128)} %get-tuple-element.5) | data formatting | bytes 2048

commit v2 on v1

--- a/solution.py
+++ b/solution.py
@@ -34,7 +34,21 @@
     return jnp.where(mask, 1.0, 0.0).astype(BF16)
 
 
-def kernel(sizes, blocks, basis_bt, basis_at, sketch, transfer, coefficients, *scratch):
+def farthest_first(n):
+    return sorted(range(1, n), key=lambda d: -min(d, n - d))
+
+
+def nearest_first(n):
+    return sorted(range(1, n), key=lambda d: min(d, n - d))
+
+
+def finish(scale, rows, inverse, transfer, coefficients):
+    out = dot(rows[:, 0:64], inverse[:, 0:64], CONTRACT_LAST, lax.Precision.HIGHEST)
+    transfer[...] = out[0:8] * scale
+    coefficients[...] = out[8:12]
+
+
+def kernel(sizes, blocks, basis_b_in, basis_a_in, sketch_in, rows_out, inverse_out, *scratch):
     X, Y, Z = sizes
     ZC = Z * 2
     YL = max(Y // 2, 1)
@@ -42,8 +56,8 @@
     FX = chips * 8
     FC = FX // 8
     (block_in, wide_n, packed, packed_in, s_own, s_zc, s_y, s_all, t_out, t_in, sp_out, sp_in, z_out, z_in,
-     mz, s_full, m_to, m_from, w_rows, gram_out, gram_in, y_out, y_in, y2_out, y2_in, x_mat,
-     in_sem, s_a, r_a, s_b, r_b, s_p, r_p, s_t, r_t, s_z1, r_z1, s_y1, r_y1, s_z2, r_z2, s_x1, r_x1,
+     mz, s_full, m_to, m_from, w_rows, gram_out, gram_in, y_out, y_in, y2_out, y2_in, basis_bt, basis_at, sketch,
+     in_sem, small_sem, s_a, r_a, s_b, r_b, s_p, r_p, s_t, r_t, s_z1, r_z1, s_y1, r_y1, s_z2, r_z2, s_x1, r_x1,
      s_g, r_g, s_yz, r_yz, s_yy, r_yy) = scratch
 
     wide = lax.axis_index("wide")
@@ -71,15 +85,10 @@
         for copy in copies:
             copy.wait_recv()
 
-    zc_peers = [(dc, dz) for dc in range(2) for dz in range(Z) if dc or dz]
-    yc_peers = [(dc, dy) for dc in range(2) for dy in range(Y) if dc or dy]
-    xc_peers = [(dc, dx) for dc in range(2) for dx in range(X) if dc or dx]
-
-    loads = [
-        pltpu.make_async_copy(blocks.at[pl.ds(i * FX, FX)], block_in.at[i], in_sem.at[i]) for i in range(8)
-    ]
-    for load in loads:
-        load.start()
+    far_z, far_y, far_x = farthest_first(Z), farthest_first(Y), farthest_first(X)
+    zc_peers = [(dc, dz) for dz in far_z + [0] for dc in range(2) if dc or dz]
+    yc_peers = [(dc, dy) for dy in far_y + [0] for dc in range(2) if dc or dy]
+    xc_peers = [(dc, dx) for dx in far_x + [0] for dc in range(2) if dc or dx]
 
     barrier = pltpu.get_barrier_semaphore()
     met = 0
@@ -95,7 +104,20 @@
             pl.semaphore_signal(barrier, inc=1, device_id=at(dx=dx, dc=dc), device_id_type=MESH)
             met += 1
 
+    small = [
+        pltpu.make_async_copy(src, dst, small_sem.at[i])
+        for i, (src, dst) in enumerate(((sketch_in, sketch), (basis_b_in, basis_bt), (basis_a_in, basis_at)))
+    ]
+    for load in small:
+        load.start()
+    loads = [
+        pltpu.make_async_copy(blocks.at[pl.ds(i * FX, FX)], block_in.at[i], in_sem.at[i]) for i in range(8)
+    ]
+    for load in loads:
+        load.start()
+
     twice = one_hot(iota((64, 128), 1) % 64 == iota((64, 128), 0))
+    small[0].wait()
     s_mine = dot(sketch[...], twice)
     s_own[...] = s_mine
     zc = z * 2 + core
@@ -106,6 +128,7 @@
         send(s_own, s_zc.at[zc], s_a.at[dc, dz], r_a.at[dc, dz], at(dz=dz, dc=dc)) for dc, dz in zc_peers
     ]
 
+    small[1].wait()
     basis2 = jnp.concatenate([basis_bt[...], basis_bt[...]], axis=0)
 
     def narrow(i, carry):
@@ -131,11 +154,13 @@
     hi = jnp.concatenate([s_zc[half + i] for i in range(half)], axis=0)
     rows_h = half * 4
     s_y[y] = jnp.where(low_half((rows_h, 128)), lo, hi).astype(BF16)
-    got_b = [send(s_y.at[y], s_y.at[y], s_b.at[dy], r_b.at[dy], at(dy=dy)) for dy in range(1, Y)]
+    got_b = [send(s_y.at[y], s_y.at[y], s_b.at[dy], r_b.at[dy], at(dy=dy)) for dy in far_y]
 
     lax.fori_loop(4, 8, narrow, 0)
     partner = at(dc=1)
     got_p = send(packed.at[1 - core], packed_in, s_p, r_p, partner)
+
+    small[2].wait()
 
     AB = min(chips * 16, 128)
     base = pl.multiple_of((chip * 16 // AB) * AB, AB)
@@ -211,14 +236,14 @@
         sp_out[i] = part[i * RZ : (i + 1) * RZ].astype(BF16)
 
     got = [
-        send(sp_out.at[(z + dz) % Z], sp_in.at[dz], s_z1.at[dz], r_z1.at[dz], at(dz=dz)) for dz in range(1, Z)
+        send(sp_out.at[(z + dz) % Z], sp_in.at[dz], s_z1.at[dz], r_z1.at[dz], at(dz=dz)) for dz in far_z
     ]
     total = sp_out[z].astype(F32)
     receive(got)
     for dz in range(1, Z):
         total = total + sp_in[dz].astype(F32)
     z_out[...] = total.astype(BF16)
-    got = [send(z_out, z_in.at[dy], s_y1.at[dy], r_y1.at[dy], at(dy=dy)) for dy in range(1, Y)]
+    got = [send(z_out, z_in.at[dy], s_y1.at[dy], r_y1.at[dy], at(dy=dy)) for dy in far_y]
     receive(got)
     for dy in range(1, Y):
         total = total + z_in[dy].astype(F32)
@@ -226,18 +251,16 @@
         mz[i] = total[i * 4 : i * 4 + 4]
     s_full[x, z] = total.astype(BF16)
     spot = s_full.at[x, z]
-    got = [send(spot, spot, s_z2.at[dz], r_z2.at[dz], at(dz=dz)) for dz in range(1, Z)]
-    receive(got)
-    spot = s_full.at[x]
-    got = [send(spot, spot, s_x1.at[dx], r_x1.at[dx], at(dx=dx)) for dx in range(1, X)]
-    receive(got)
-
+    got = {dz: send(spot, spot, s_z2.at[dz], r_z2.at[dz], at(dz=dz)) for dz in far_z}
+    got_x = []
+    for dz in [0] + nearest_first(Z):
+        if dz:
+            receive([got[dz]])
+        spot = s_full.at[x, (z + Z - dz) % Z]
+        for dx in far_x:
+            got_x.append(send(spot, spot, s_x1.at[dx, dz], r_x1.at[dx, dz], at(dx=dx)))
+    receive(got_x)
     s_x = [s_full[i].reshape(MR, 128) for i in range(X)]
-    big = dot(s_x[0], s_x[0], CONTRACT_FIRST)
-    for i in range(1, X):
-        big = big + dot(s_x[i], s_x[i], CONTRACT_FIRST)
-    gram_out[...] = swap_halves(big[0:64]) + big[64:128]
-    got_g = send(gram_out, gram_in, s_g, r_g, partner)
 
     low = low_half((MR, 128))
     rhs = []
@@ -264,12 +287,16 @@
     ylow = dot(packed[core, 0 : FX // 2, :], w0) + dot(packed_in[0 : FX // 2, :], w1)
     yhigh = dot(packed[core, FX // 2 : FX, :], w0) + dot(packed_in[FX // 2 : FX, :], w1)
     ypart = jnp.where(low_half((FX // 2, 128)), ylow, yhigh)
-    for i in range(YL):
-        for j in range(Z):
-            y_out[j, i] = ypart[(i * Z + j) * 8 : (i * Z + j) * 8 + 8]
-    got_y = [
-        send(y_out.at[(z + dz) % Z], y_in.at[dz], s_yz.at[dz], r_yz.at[dz], at(dz=dz)) for dz in range(1, Z)
-    ]
+    for j in range(Z):
+        block = [ypart[(i * Z + j) * 8 : (i * Z + j) * 8 + 8] for i in range(YL)]
+        y_out[j] = jnp.concatenate(block, axis=0).astype(BF16)
+    got_y = [send(y_out.at[(z + dz) % Z], y_in.at[dz], s_yz.at[dz], r_yz.at[dz], at(dz=dz)) for dz in far_z]
+
+    big = dot(s_x[0], s_x[0], CONTRACT_FIRST)
+    for i in range(1, X):
+        big = big + dot(s_x[i], s_x[i], CONTRACT_FIRST)
+    gram_out[...] = swap_halves(big[0:64]) + big[64:128]
+    got_g = send(gram_out, gram_in, s_g, r_g, partner)
 
     receive([got_g])
     g = gram_out[...] + gram_in[...]
@@ -278,27 +305,44 @@
     tiles = [g[i * 8 : i * 8 + 8] for i in range(8)]
     sub = iota((8, 128), 0)
 
+    def lane(v, j):
+        return jnp.broadcast_to(v[:, 64 + j : 65 + j], v.shape)
+
     def eliminate(tiles, first, last):
-        for j in range(first, last):
-            pos = j % 8
-            line = tiles[j // 8][pos : pos + 1]
-            line_scaled = line / line[:, 64 + j : 65 + j]
-            for i in range(j // 8, 8):
-                c = tiles[i][:, 64 + j : 65 + j]
-                if i == j // 8:
-                    c = jnp.where(sub[:, 0:1] > pos, c, 0.0)
-                tiles[i] = tiles[i] - c * line_scaled
+        for j in range(first, last, 4):
+            home, pos = j // 8, j % 8
+            lines = [tiles[home][pos + t : pos + t + 1] for t in range(4)]
+            u = [[lane(lines[t], j + v) for v in range(4)] for t in range(4)]
+            inv = []
+            for t in range(4):
+                inv.append(1.0 / u[t][t])
+                for v in range(t + 1, 4):
+                    ratio = u[t][v] * inv[t]
+                    for w in range(v, 4):
+                        u[v][w] = u[v][w] - ratio * u[t][w]
+                    lines[v] = lines[v] - ratio * lines[t]
+            for i in range(home, 8):
+                c = [lane(tiles[i], j + v) for v in range(4)]
+                new = tiles[i]
+                for t in range(4):
+                    m = c[t] * inv[t]
+                    if i == home:
+                        m = jnp.where(sub > pos + t, m, 0.0)
+                    for v in range(t + 1, 4):
+                        c[v] = c[v] - m * u[t][v]
+                    new = new - m * lines[t]
+                tiles[i] = new
         return tiles
 
-    tiles = eliminate(tiles, 0, 24)
+    tiles = eliminate(tiles, 0, 32)
 
     receive(got_y)
-    acc = y_out[z]
+    acc = y_out[z].astype(F32)
     for dz in range(1, Z):
-        acc = acc + y_in[dz]
+        acc = acc + y_in[dz].astype(F32)
     for i in range(YL):
         for cc in range(2):
-            y2_out[i, cc] = acc[i, cc * 4 : cc * 4 + 4]
+            y2_out[i, cc] = acc[i * 8 + cc * 4 : i * 8 + cc * 4 + 4]
     got_y = [
         send(
             y2_out.at[((y + dy) % Y) % YL, (core + dc) % 2],
@@ -309,12 +353,11 @@
         )
         for dc, dy in yc_peers
     ]
-    tiles = eliminate(tiles, 24, 64)
-    x_mat[...] = jnp.concatenate(tiles, axis=0)
-    elim = x_mat[...]
+    tiles = eliminate(tiles, 32, 64)
+    elim = jnp.concatenate(tiles, axis=0)
     diagonal = jnp.where(iota((64, 128), 1) == iota((64, 128), 0) + 64, elim, 0.0)
     pivots = jnp.sum(diagonal, axis=1, keepdims=True)
-    inverse = elim[:, 0:64] * (1.0 / jnp.sqrt(pivots))
+    inverse_out[...] = elim * (1.0 / jnp.sqrt(pivots))
 
     receive(got_y)
     acc = y2_out[y % YL, core]
@@ -322,10 +365,7 @@
         acc = acc + y2_in[dc, dy]
     acc = jnp.where(y // YL == 0, acc, swap_halves(acc)) if Y > 1 else acc
     s_mine = mz[y]
-    rows = jnp.concatenate([s_mine, swap_halves(s_mine), acc, acc], axis=0)
-    out = dot(rows[:, 0:64], inverse, CONTRACT_LAST, lax.Precision.HIGHEST)
-    transfer[...] = out[0:8] * float((chips * 64) ** 0.5)
-    coefficients[...] = out[8:12]
+    rows_out[...] = jnp.concatenate([s_mine, swap_halves(s_mine), acc, acc], axis=0)
 
     for copy in waits:
         copy.wait_send()
@@ -362,12 +402,15 @@
         pltpu.VMEM((16, 4, 8, 128), F32),
         pltpu.VMEM((64, 128), F32),
         pltpu.VMEM((64, 128), F32),
-        pltpu.VMEM((Z, YL, 8, 128), F32),
-        pltpu.VMEM((Z, YL, 8, 128), F32),
+        pltpu.VMEM((Z, YL * 8, 128), BF16),
+        pltpu.VMEM((Z, YL * 8, 128), BF16),
         pltpu.VMEM((YL, 2, 4, 128), F32),
         pltpu.VMEM((2, Y, 4, 128), F32),
-        pltpu.VMEM((64, 128), F32),
+        pltpu.VMEM((64, cb), BF16),
+        pltpu.VMEM((chips, chips * 16), BF16),
+        pltpu.VMEM((4, 64), BF16),
         dma((8,)),
+        dma((3,)),
         dma((2, Z)), dma((2, Z)),
         dma((Y,)), dma((Y,)),
         dma, dma,
@@ -375,7 +418,7 @@
         dma((Z,)), dma((Z,)),
         dma((Y,)), dma((Y,)),
         dma((Z,)), dma((Z,)),
-        dma((X,)), dma((X,)),
+        dma((X, Z)), dma((X, Z)),
         dma, dma,
         dma((Z,)), dma((Z,)),
         dma((2, Y)), dma((2, Y)),
@@ -385,15 +428,24 @@
 def per_device(sizes, blocks, basis_a, basis_b, sketch):
     fibres, own_a, cb = blocks.shape
     vmem = pl.BlockSpec(memory_space=pltpu.VMEM)
-    return pl.pallas_call(
+    anywhere = pl.BlockSpec(memory_space=pl.ANY)
+    rows, inverse = pl.pallas_call(
         functools.partial(kernel, sizes),
-        out_shape=(jax.ShapeDtypeStruct((8, 64), F32), jax.ShapeDtypeStruct((4, 64), F32)),
-        in_specs=[pl.BlockSpec(memory_space=pl.ANY), vmem, vmem, vmem],
+        out_shape=(jax.ShapeDtypeStruct((16, 128), F32), jax.ShapeDtypeStruct((64, 128), F32)),
+        in_specs=[anywhere] * 4,
         out_specs=(vmem, vmem),
         scratch_shapes=scratch_for(sizes, cb),
         compiler_params=pltpu.CompilerParams(collective_id=0, has_side_effects=True),
         name="tucker",
     )(blocks.reshape(fibres * own_a, cb), basis_b.T, basis_a.T, sketch)
+    chips = sizes[1] * sizes[2]
+    return pl.pallas_call(
+        functools.partial(finish, float((chips * 64) ** 0.5)),
+        out_shape=(jax.ShapeDtypeStruct((8, 64), F32), jax.ShapeDtypeStruct((4, 64), F32)),
+        in_specs=[vmem, vmem],
+        out_specs=(vmem, vmem),
+        name="finish",
+    )(rows, inverse)
 
 
 def solution(mesh):

time: 69.8 us -> 63.4 us (0.908)
  Pallas kernels: 66.5 us -> 62.5 us
  local copies, waits for them, and re-layouts: 2.5 us -> 0 us
    pallas_call x1, Pallas kernels: 66.5 us -> 61 us  [per_device(): pl.pallas_call(functools.partial(kernel, sizes), out_shape=(jax.ShapeDtyp...]
    unnamed x2 -> x0, local copies, waits for them, and re-layouts: 2.5 us -> none
    pallas_call x0 -> x1, Pallas kernels: none -> 1.54 us  [per_device(): pl.pallas_call(functools.partial(finish, float((chips * 64) ** 0.5)), out...]
where the time goes in v2:
time: 63.4 us; the launch traced here: 63.2 us
  Pallas kernels  62.5 us (99%)
  between operations  0.64 us (1%)
    pallas_call x1, Pallas kernels, per_device(): pl.pallas_call(functools.partial(kernel, sizes), out_shape=(jax.ShapeDtyp...  61 us
    pallas_call x1, Pallas kernels, per_device(): pl.pallas_call(functools.partial(finish, float((chips * 64) ** 0.5)), out...  1.54 us

profile of v2, /device:TPU:1, one launch (start us, length us, event | category | flops | bytes accessed | tf_op | source)
XLA Modules:
  0.0 63.2 jit_solution(11681645730590438246)
XLA Ops:
  0.6 61.0 %tucker.1 = (f32[16,128]{1,0:T(8,128)}, f32[64,128]{1,0:T(8,128)}) custom-call(bf16[4096,512]{1,0:T(8,128)(2,1)} %bitcast.3, bf16[64,512]{1,0:T(8,128)(2,1)} %bitcast.5, bf16[64,1024]{1,0:T(8,128)(2,1)} %bitcast.4, bf16[4,64]{1,0:T(4,128)(2,1)} %sketch_in.1), custom_call_target="tpu_custom_call" | custom-call | tf_op jit(solution)/shard_map/tucker/pallas_call | solution.py:432
  61.6 1.5 %finish.1 = (f32[8,64]{1,0:T(8,128)}, f32[4,64]{1,0:T(4,128)}) custom-call(f32[16,128]{1,0:T(8,128)} %get-tuple-element.4.rows, f32[64,128]{1,0:T(8,128)} %get-tuple-element.5.inverse), custom_call_target="tpu_custom_call" | custom-call | tf_op jit(solution)/shard_map/finish/pallas_call | solution.py:442

commit v3 on v2

--- a/solution.py
+++ b/solution.py
@@ -51,14 +51,15 @@
 def kernel(sizes, blocks, basis_b_in, basis_a_in, sketch_in, rows_out, inverse_out, *scratch):
     X, Y, Z = sizes
     ZC = Z * 2
-    YL = max(Y // 2, 1)
+    ZL = Z // 2
     chips = Y * Z
     FX = chips * 8
-    FC = FX // 8
-    (block_in, wide_n, packed, packed_in, s_own, s_zc, s_y, s_all, t_out, t_in, sp_out, sp_in, z_out, z_in,
-     mz, s_full, m_to, m_from, w_rows, gram_out, gram_in, y_out, y_in, y2_out, y2_in, basis_bt, basis_at, sketch,
-     in_sem, small_sem, s_a, r_a, s_b, r_b, s_p, r_p, s_t, r_t, s_z1, r_z1, s_y1, r_y1, s_z2, r_z2, s_x1, r_x1,
-     s_g, r_g, s_yz, r_yz, s_yy, r_yy) = scratch
+    FC = FX // Y
+    RC = FC * 8
+    (block_in, wide_n, packed, n_in, s_own, s_zc, s_y, s_all, t_out, t_in, sp_out, sp_in, z_out, z_in,
+     mz, s_full, m_to, m_from, gram_out, gram_in, y_out, y_in, basis_bt, basis_at, sketch,
+     in_sem, small_sem, s_a, r_a, s_b, r_b, s_n, r_n, s_t, r_t, s_z1, r_z1, s_y1, r_y1, s_z2, r_z2, s_x1, r_x1,
+     s_g, r_g, s_y1z, r_y1z) = scratch
 
     wide = lax.axis_index("wide")
     x = lax.axis_index("pair")
@@ -72,18 +73,25 @@
         return (row * 2 + (core + dc) % 2, (x + dx) % X)
 
     waits = []
-
-    def send(src, dst, ssem, rsem, peer):
+    slow_waits = []
+
+    def send(src, dst, ssem, rsem, peer, slow=False):
         copy = pltpu.make_async_remote_copy(
             src_ref=src, dst_ref=dst, send_sem=ssem, recv_sem=rsem, device_id=peer, device_id_type=MESH
         )
         copy.start()
-        waits.append(copy)
+        (slow_waits if slow else waits).append(copy)
         return copy
 
     def receive(copies):
-        for copy in copies:
+        for copy in reversed(copies):
             copy.wait_recv()
+
+    def drain(keep=0):
+        done = waits[: len(waits) - keep]
+        for copy in done:
+            copy.wait_send()
+        del waits[: len(done)]
 
     far_z, far_y, far_x = farthest_first(Z), farthest_first(Y), farthest_first(X)
     zc_peers = [(dc, dz) for dz in far_z + [0] for dc in range(2) if dc or dz]
@@ -111,7 +119,7 @@
     for load in small:
         load.start()
     loads = [
-        pltpu.make_async_copy(blocks.at[pl.ds(i * FX, FX)], block_in.at[i], in_sem.at[i]) for i in range(8)
+        pltpu.make_async_copy(blocks.at[pl.ds(i * RC, RC)], block_in.at[i], in_sem.at[i]) for i in range(Y)
     ]
     for load in loads:
         load.start()
@@ -122,19 +130,12 @@
     s_own[...] = s_mine
     zc = z * 2 + core
     s_zc[zc] = s_mine
-    pl.semaphore_wait(barrier, met)
-
-    got_a = [
-        send(s_own, s_zc.at[zc], s_a.at[dc, dz], r_a.at[dc, dz], at(dz=dz, dc=dc)) for dc, dz in zc_peers
-    ]
-
     small[1].wait()
     basis2 = jnp.concatenate([basis_bt[...], basis_bt[...]], axis=0)
 
     def narrow(i, carry):
-        pltpu.make_async_copy(blocks.at[pl.ds(i * FX, FX)], block_in.at[i], in_sem.at[i]).wait()
+        pltpu.make_async_copy(blocks.at[pl.ds(i * RC, RC)], block_in.at[i], in_sem.at[i]).wait()
         wide_n[...] = dot(block_in[i], basis2, CONTRACT_LAST)
-        rows = pl.ds(pl.multiple_of(i * FC, FC), FC)
         low = low_half((FC, 128))
         odd = (iota((FC, 128), 1) // 32) % 2 == 1
         for t in range(2):
@@ -142,11 +143,18 @@
             first = jnp.where(low, part[0], part[2])
             second = jnp.where(low, part[1], part[3])
             lanes = slice(t * 128, t * 128 + 128)
-            packed[0, rows, lanes] = jnp.where(odd, pltpu.roll(second, 32, 1), first).astype(BF16)
-            packed[1, rows, lanes] = jnp.where(odd, second, pltpu.roll(first, 96, 1)).astype(BF16)
+            packed[0, i, :, lanes] = jnp.where(odd, pltpu.roll(second, 32, 1), first).astype(BF16)
+            packed[1, i, :, lanes] = jnp.where(odd, second, pltpu.roll(first, 96, 1)).astype(BF16)
         return carry
 
-    lax.fori_loop(0, 4, narrow, 0)
+    lax.fori_loop(0, Y // 2, narrow, 0)
+    pl.semaphore_wait(barrier, met)
+
+    got_a = [
+        send(s_own, s_zc.at[zc], s_a.at[dc, dz], r_a.at[dc, dz], at(dz=dz, dc=dc)) for dc, dz in zc_peers
+    ]
+
+    lax.fori_loop(Y // 2, Y, narrow, 0)
 
     receive(got_a)
     half = ZC // 2
@@ -156,24 +164,20 @@
     s_y[y] = jnp.where(low_half((rows_h, 128)), lo, hi).astype(BF16)
     got_b = [send(s_y.at[y], s_y.at[y], s_b.at[dy], r_b.at[dy], at(dy=dy)) for dy in far_y]
 
-    lax.fori_loop(4, 8, narrow, 0)
     partner = at(dc=1)
-    got_p = send(packed.at[1 - core], packed_in, s_p, r_p, partner)
-
     small[2].wait()
 
-    AB = min(chips * 16, 128)
-    base = pl.multiple_of((chip * 16 // AB) * AB, AB)
-    a_part = basis_at[:, pl.ds(base, AB)]
+    ZA = Z * 16
+    a_part = basis_at[:, pl.ds(pl.multiple_of(y * ZA, ZA), ZA)]
     MR = chips * 4
 
     def chip_of(index):
         zy = index // 4
         return (zy % Y) * Z + zy // Y
 
-    col = iota((AB, 256), 1)
-    pick = base + iota((AB, 256), 0) == (
-        chip * 16 + ((core + (col // 32) % 2) % 2) * 8 + ((col // 8) % 4) * 2 + (col // 64) % 2
+    col = iota((ZA, 256), 1)
+    pick = iota((ZA, 256), 0) == (
+        z * 16 + ((core + (col // 32) % 2) % 2) * 8 + ((col // 8) % 4) * 2 + (col // 64) % 2
     )
     a_cols = dot(a_part, one_hot(pick)).astype(BF16)
     spread = one_hot(chip_of(iota((MR, chips), 0)) == iota((MR, chips), 1))
@@ -181,14 +185,6 @@
     for rh in range(2):
         keep = iota((MR, 256), 1) % 8 == rh * 4 + iota((MR, 256), 0) % 4
         m_to[rh] = jnp.where(keep, rows_a, 0.0).astype(BF16)
-    row = iota((128, AB), 0)
-    pick = base + iota((128, AB), 1) == chip * 16 + ((core + row // 64) % 2) * 8 + (row // 8) % 8
-    a_rows = dot(one_hot(pick), a_part, CONTRACT_LAST).astype(BF16)
-    spread = one_hot(chip_of(iota((chips, MR), 1)) == iota((chips, MR), 0))
-    cols_a = dot(a_rows, spread)
-    for rh in range(2):
-        keep = iota((128, MR), 0) % 8 == rh * 4 + iota((128, MR), 1) % 4
-        m_from[:, rh * MR : (rh + 1) * MR] = jnp.where(keep, cols_a, 0.0).astype(BF16)
 
     receive(got_b)
     low = low_half((rows_h, 128))
@@ -200,7 +196,7 @@
 
     low = low_half((32, 128))
     for cc in range(2):
-        t = dot(packed[cc], s_all[...], CONTRACT_FIRST)
+        t = dot(packed[cc].reshape(FX, 256), s_all[...], CONTRACT_FIRST)
         for ah in range(4):
             pair = jnp.where(low, t[ah * 64 : ah * 64 + 32], t[ah * 64 + 32 : ah * 64 + 64])
             for xx in range(4):
@@ -215,13 +211,29 @@
         )
         for dc, dx in xc_peers
     ]
+    def spread_fibres(peers):
+        return [
+            send(
+                packed.at[(core + dc) % 2, (y + dy) % Y],
+                n_in.at[dc, dy],
+                s_n.at[dc, dy],
+                r_n.at[dc, dy],
+                at(dy=dy, dc=dc),
+                slow=True,
+            )
+            for dc, dy in peers
+        ]
+
+    got_n = spread_fibres([p for p in yc_peers if p[0] == 0])
     mine = t_out[core, x]
-    receive(got_t)
-    for dx in range(1, X):
-        mine = mine + t_in[0, dx]
-    other = t_in[1, 0]
-    for dx in range(1, X):
-        other = other + t_in[1, dx]
+    other = None
+    drain(len(got_t))
+    for (dc, dx), copy in reversed(list(zip(xc_peers, got_t))):
+        copy.wait_recv()
+        if dc == 0:
+            mine = mine + t_in[0, dx]
+        else:
+            other = t_in[1, dx] if other is None else other + t_in[1, dx]
     u = jnp.concatenate([mine.reshape(32, 128), other.reshape(32, 128)], axis=0)
     low = low_half((64, 128))
     v = swap_halves(u)
@@ -239,28 +251,52 @@
         send(sp_out.at[(z + dz) % Z], sp_in.at[dz], s_z1.at[dz], r_z1.at[dz], at(dz=dz)) for dz in far_z
     ]
     total = sp_out[z].astype(F32)
-    receive(got)
-    for dz in range(1, Z):
+    drain(len(got))
+
+    row = iota((128, ZA), 0)
+    pick = one_hot(iota((128, ZA), 1) == z * 16 + ((core + row // 64) % 2) * 8 + (row // 8) % 8)
+    spread = one_hot(chip_of(iota((chips, MR), 1)) == iota((chips, MR), 0))
+    for dy in range(Y):
+        a_part = basis_at[:, pl.ds(pl.multiple_of(((y + Y - dy) % Y) * ZA, ZA), ZA)]
+        cols_a = dot(dot(pick, a_part, CONTRACT_LAST).astype(BF16), spread)
+        for rh in range(2):
+            keep = iota((128, MR), 0) % 8 == rh * 4 + iota((128, MR), 1) % 4
+            m_from[dy * 128 : dy * 128 + 128, rh * MR : (rh + 1) * MR] = jnp.where(keep, cols_a, 0.0).astype(BF16)
+
+    for dz, copy in reversed(list(zip(far_z, got))):
+        copy.wait_recv()
         total = total + sp_in[dz].astype(F32)
     z_out[...] = total.astype(BF16)
     got = [send(z_out, z_in.at[dy], s_y1.at[dy], r_y1.at[dy], at(dy=dy)) for dy in far_y]
-    receive(got)
-    for dy in range(1, Y):
+    drain(len(got))
+    for dy, copy in reversed(list(zip(far_y, got))):
+        copy.wait_recv()
         total = total + z_in[dy].astype(F32)
     for i in range(Y):
         mz[i] = total[i * 4 : i * 4 + 4]
     s_full[x, z] = total.astype(BF16)
     spot = s_full.at[x, z]
     got = {dz: send(spot, spot, s_z2.at[dz], r_z2.at[dz], at(dz=dz)) for dz in far_z}
+    got_n += spread_fibres([p for p in yc_peers if p[0] == 1])
     got_x = []
+    drain(len(got))
     for dz in [0] + nearest_first(Z):
         if dz:
             receive([got[dz]])
         spot = s_full.at[x, (z + Z - dz) % Z]
         for dx in far_x:
             got_x.append(send(spot, spot, s_x1.at[dx, dz], r_x1.at[dx, dz], at(dx=dx)))
-    receive(got_x)
+    drain(len(got_x))
+    receive(got_n)
+    for i in range(0, len(got_x), len(far_x)):
+        receive(got_x[i : i + len(far_x)])
     s_x = [s_full[i].reshape(MR, 128) for i in range(X)]
+
+    big = dot(s_x[0], s_x[0], CONTRACT_FIRST)
+    for i in range(1, X):
+        big = big + dot(s_x[i], s_x[i], CONTRACT_FIRST)
+    gram_out[...] = swap_halves(big[0:64]) + big[64:128]
+    got_g = send(gram_out, gram_in, s_g, r_g, partner)
 
     low = low_half((MR, 128))
     rhs = []
@@ -272,31 +308,35 @@
                 [jnp.where(low, s0, swap_halves(s1)), jnp.where(low, swap_halves(s0), s1)], axis=0
             ).astype(BF16)
         )
+    w = dot(m_from[...], jnp.concatenate(rhs, axis=1))
     low = low_half((128, 128))
-    for xp in range(X // 2):
-        w = dot(m_from[...], rhs[xp])
-        v = swap_halves(w)
-        even = jnp.where(low, w, v)
-        odd = jnp.where(low, v, w)
-        for a in range(16):
-            w_rows[a, 2 * xp] = even[a * 8 : a * 8 + 8]
-            w_rows[a, 2 * xp + 1] = odd[a * 8 : a * 8 + 8]
-    receive([got_p])
-    w0 = w_rows[0:8].reshape(256, 128).astype(BF16)
-    w1 = w_rows[8:16].reshape(256, 128).astype(BF16)
-    ylow = dot(packed[core, 0 : FX // 2, :], w0) + dot(packed_in[0 : FX // 2, :], w1)
-    yhigh = dot(packed[core, FX // 2 : FX, :], w0) + dot(packed_in[FX // 2 : FX, :], w1)
-    ypart = jnp.where(low_half((FX // 2, 128)), ylow, yhigh)
-    for j in range(Z):
-        block = [ypart[(i * Z + j) * 8 : (i * Z + j) * 8 + 8] for i in range(YL)]
-        y_out[j] = jnp.concatenate(block, axis=0).astype(BF16)
-    got_y = [send(y_out.at[(z + dz) % Z], y_in.at[dz], s_yz.at[dz], r_yz.at[dz], at(dz=dz)) for dz in far_z]
-
-    big = dot(s_x[0], s_x[0], CONTRACT_FIRST)
-    for i in range(1, X):
-        big = big + dot(s_x[i], s_x[i], CONTRACT_FIRST)
-    gram_out[...] = swap_halves(big[0:64]) + big[64:128]
-    got_g = send(gram_out, gram_in, s_g, r_g, partner)
+    ypart = None
+    for dy in range(Y):
+        by_x = []
+        for xp in range(X // 2):
+            v = w[dy * 128 : dy * 128 + 128, xp * 128 : xp * 128 + 128]
+            t = swap_halves(v)
+            by_x += [jnp.where(low, v, t), jnp.where(low, t, v)]
+        for dc in range(2):
+            tiles = [by_x[xx][a * 8 : a * 8 + 8] for a in range(dc * 8, dc * 8 + 8) for xx in range(X)]
+            w_rows = jnp.concatenate(tiles, axis=0).astype(BF16)
+            fibres = n_in[dc, dy] if dc or dy else packed[core, y]
+            term = dot(fibres, w_rows)
+            ypart = term if ypart is None else ypart + term
+    ypart = jnp.where(low_half((FC // 2, 128)), ypart[0 : FC // 2], ypart[FC // 2 : FC])
+    for i in range(ZL):
+        for cc in range(2):
+            y_out[i, cc] = ypart[i * 8 + cc * 4 : i * 8 + cc * 4 + 4]
+    got_y = [
+        send(
+            y_out.at[((z + dz) % Z) % ZL, (core + dc) % 2],
+            y_in.at[dc, dz],
+            s_y1z.at[dc, dz],
+            r_y1z.at[dc, dz],
+            at(dz=dz, dc=dc),
+        )
+        for dc, dz in zc_peers
+    ]
 
     receive([got_g])
     g = gram_out[...] + gram_in[...]
@@ -334,57 +374,39 @@
                 tiles[i] = new
         return tiles
 
-    tiles = eliminate(tiles, 0, 32)
-
-    receive(got_y)
-    acc = y_out[z].astype(F32)
-    for dz in range(1, Z):
-        acc = acc + y_in[dz].astype(F32)
-    for i in range(YL):
-        for cc in range(2):
-            y2_out[i, cc] = acc[i * 8 + cc * 4 : i * 8 + cc * 4 + 4]
-    got_y = [
-        send(
-            y2_out.at[((y + dy) % Y) % YL, (core + dc) % 2],
-            y2_in.at[dc, dy],
-            s_yy.at[dc, dy],
-            r_yy.at[dc, dy],
-            at(dy=dy, dc=dc),
-        )
-        for dc, dy in yc_peers
-    ]
-    tiles = eliminate(tiles, 32, 64)
+    tiles = eliminate(tiles, 0, 64)
     elim = jnp.concatenate(tiles, axis=0)
     diagonal = jnp.where(iota((64, 128), 1) == iota((64, 128), 0) + 64, elim, 0.0)
     pivots = jnp.sum(diagonal, axis=1, keepdims=True)
     inverse_out[...] = elim * (1.0 / jnp.sqrt(pivots))
 
-    receive(got_y)
-    acc = y2_out[y % YL, core]
-    for dc, dy in yc_peers:
-        acc = acc + y2_in[dc, dy]
-    acc = jnp.where(y // YL == 0, acc, swap_halves(acc)) if Y > 1 else acc
+    drain()
+    for copy in slow_waits:
+        copy.wait_send()
+    acc = y_out[z % ZL, core]
+    for (dc, dz), copy in reversed(list(zip(zc_peers, got_y))):
+        copy.wait_recv()
+        acc = acc + y_in[dc, dz]
+    acc = jnp.where(z // ZL == 0, acc, swap_halves(acc))
     s_mine = mz[y]
     rows_out[...] = jnp.concatenate([s_mine, swap_halves(s_mine), acc, acc], axis=0)
-
-    for copy in waits:
-        copy.wait_send()
 
 
 def scratch_for(sizes, cb):
     X, Y, Z = sizes
     ZC = Z * 2
-    YL = max(Y // 2, 1)
+    ZL = Z // 2
     chips = Y * Z
     FX = chips * 8
+    FC = FX // Y
     MR = chips * 4
     RZ = Y * 4
     dma = pltpu.SemaphoreType.DMA
     return [
-        pltpu.VMEM((8, FX, cb), BF16),
-        pltpu.VMEM((FX, 128), F32),
-        pltpu.VMEM((2, FX, 256), BF16),
-        pltpu.VMEM((FX, 256), BF16),
+        pltpu.VMEM((Y, FC * 8, cb), BF16),
+        pltpu.VMEM((FC * 8, 128), F32),
+        pltpu.VMEM((2, Y, FC, 256), BF16),
+        pltpu.VMEM((2, Y, FC, 256), BF16),
         pltpu.VMEM((4, 128), F32),
         pltpu.VMEM((ZC, 4, 128), F32),
         pltpu.VMEM((Y, ZC * 2, 128), BF16),
@@ -398,30 +420,26 @@
         pltpu.VMEM((Y, 4, 128), F32),
         pltpu.VMEM((X, Z, RZ, 128), BF16),
         pltpu.VMEM((2, MR, 256), BF16),
-        pltpu.VMEM((128, 2 * MR), BF16),
-        pltpu.VMEM((16, 4, 8, 128), F32),
+        pltpu.VMEM((Y * 128, 2 * MR), BF16),
         pltpu.VMEM((64, 128), F32),
         pltpu.VMEM((64, 128), F32),
-        pltpu.VMEM((Z, YL * 8, 128), BF16),
-        pltpu.VMEM((Z, YL * 8, 128), BF16),
-        pltpu.VMEM((YL, 2, 4, 128), F32),
-        pltpu.VMEM((2, Y, 4, 128), F32),
+        pltpu.VMEM((ZL, 2, 4, 128), F32),
+        pltpu.VMEM((2, Z, 4, 128), F32),
         pltpu.VMEM((64, cb), BF16),
         pltpu.VMEM((chips, chips * 16), BF16),
         pltpu.VMEM((4, 64), BF16),
-        dma((8,)),
+        dma((Y,)),
         dma((3,)),
         dma((2, Z)), dma((2, Z)),
         dma((Y,)), dma((Y,)),
-        dma, dma,
+        dma((2, Y)), dma((2, Y)),
         dma((2, X)), dma((2, X)),
         dma((Z,)), dma((Z,)),
         dma((Y,)), dma((Y,)),
         dma((Z,)), dma((Z,)),
         dma((X, Z)), dma((X, Z)),
         dma, dma,
-        dma((Z,)), dma((Z,)),
-        dma((2, Y)), dma((2, Y)),
+        dma((2, Z)), dma((2, Z)),
     ]
 
 

time: 63.4 us -> 57.3 us (0.904)
  Pallas kernels: 62.5 us -> 56.5 us
    pallas_call x1, Pallas kernels: 61 us -> 54.9 us  [per_device(): pl.pallas_call(functools.partial(kernel, sizes), out_shape=(jax.ShapeDtyp...]
where the time goes in v3:
time: 57.3 us; the launch traced here: 57.1 us
  Pallas kernels  56.5 us (99%)
  between operations  0.64 us (1%)
    pallas_call x1, Pallas kernels, per_device(): pl.pallas_call(functools.partial(kernel, sizes), out_shape=(jax.ShapeDtyp...  54.9 us
    pallas_call x1, Pallas kernels, per_device(): pl.pallas_call(functools.partial(finish, float((chips * 64) ** 0.5)), out...  1.54 us

profile of v3, /device:TPU:1, one launch (start us, length us, event | category | flops | bytes accessed | tf_op | source)
XLA Modules:
  0.0 57.1 jit_solution(7635688868599170520)
XLA Ops:
  0.6 54.9 %tucker.1 = (f32[16,128]{1,0:T(8,128)}, f32[64,128]{1,0:T(8,128)}) custom-call(bf16[4096,512]{1,0:T(8,128)(2,1)} %bitcast.3, bf16[64,512]{1,0:T(8,128)(2,1)} %bitcast.5, bf16[64,1024]{1,0:T(8,128)(2,1)} %bitcast.4, bf16[4,64]{1,0:T(4,128)(2,1)} %sketch_in.1), custom_call_target="tpu_custom_call" | custom-call | tf_op jit(solution)/shard_map/tucker/pallas_call | solution.py:450
  55.6 1.5 %finish.1 = (f32[8,64]{1,0:T(8,128)}, f32[4,64]{1,0:T(4,128)}) custom-call(f32[16,128]{1,0:T(8,128)} %get-tuple-element.4.rows, f32[64,128]{1,0:T(8,128)} %get-tuple-element.5.inverse), custom_call_target="tpu_custom_call" | custom-call | tf_op jit(solution)/shard_map/finish/pallas_call | solution.py:460

commit v4 on v3

--- a/solution.py
+++ b/solution.py
@@ -56,7 +56,7 @@
     FX = chips * 8
     FC = FX // Y
     RC = FC * 8
-    (block_in, wide_n, packed, n_in, s_own, s_zc, s_y, s_all, t_out, t_in, sp_out, sp_in, z_out, z_in,
+    (block_in, wide_n, by_a, packed, n_in, n_x, s_own, s_zc, s_y, s_all, t_out, t_in, sp_out, sp_in, z_out, z_in,
      mz, s_full, m_to, m_from, gram_out, gram_in, y_out, y_in, basis_bt, basis_at, sketch,
      in_sem, small_sem, s_a, r_a, s_b, r_b, s_n, r_n, s_t, r_t, s_z1, r_z1, s_y1, r_y1, s_z2, r_z2, s_x1, r_x1,
      s_g, r_g, s_y1z, r_y1z) = scratch
@@ -98,6 +98,11 @@
     yc_peers = [(dc, dy) for dy in far_y + [0] for dc in range(2) if dc or dy]
     xc_peers = [(dc, dx) for dx in far_x + [0] for dc in range(2) if dc or dx]
 
+    small = [
+        pltpu.make_async_copy(src, dst, small_sem.at[i])
+        for i, (src, dst) in enumerate(((sketch_in, sketch), (basis_b_in, basis_bt), (basis_a_in, basis_at)))
+    ]
+    small[0].start()
     barrier = pltpu.get_barrier_semaphore()
     met = 0
     for dc, dz in zc_peers:
@@ -112,11 +117,7 @@
             pl.semaphore_signal(barrier, inc=1, device_id=at(dx=dx, dc=dc), device_id_type=MESH)
             met += 1
 
-    small = [
-        pltpu.make_async_copy(src, dst, small_sem.at[i])
-        for i, (src, dst) in enumerate(((sketch_in, sketch), (basis_b_in, basis_bt), (basis_a_in, basis_at)))
-    ]
-    for load in small:
+    for load in small[1:]:
         load.start()
     loads = [
         pltpu.make_async_copy(blocks.at[pl.ds(i * RC, RC)], block_in.at[i], in_sem.at[i]) for i in range(Y)
@@ -143,18 +144,17 @@
             first = jnp.where(low, part[0], part[2])
             second = jnp.where(low, part[1], part[3])
             lanes = slice(t * 128, t * 128 + 128)
-            packed[0, i, :, lanes] = jnp.where(odd, pltpu.roll(second, 32, 1), first).astype(BF16)
-            packed[1, i, :, lanes] = jnp.where(odd, second, pltpu.roll(first, 96, 1)).astype(BF16)
+            by_a[0, i, :, lanes] = jnp.where(odd, pltpu.roll(second, 32, 1), first).astype(BF16)
+            by_a[1, i, :, lanes] = jnp.where(odd, second, pltpu.roll(first, 96, 1)).astype(BF16)
         return carry
 
-    lax.fori_loop(0, Y // 2, narrow, 0)
     pl.semaphore_wait(barrier, met)
 
     got_a = [
         send(s_own, s_zc.at[zc], s_a.at[dc, dz], r_a.at[dc, dz], at(dz=dz, dc=dc)) for dc, dz in zc_peers
     ]
 
-    lax.fori_loop(Y // 2, Y, narrow, 0)
+    lax.fori_loop(0, Y, narrow, 0)
 
     receive(got_a)
     half = ZC // 2
@@ -166,6 +166,11 @@
 
     partner = at(dc=1)
     small[2].wait()
+
+    lane_in = iota((256, 256), 0)
+    move = one_hot(iota((256, 256), 1) == (lane_in // 8 % 4) * 64 + lane_in // 32 * 8 + lane_in % 8)
+    for cc in range(2):
+        packed[cc] = dot(by_a[cc].reshape(FX, 256), move).astype(BF16).reshape(Y, FC, 256)
 
     ZA = Z * 16
     a_part = basis_at[:, pl.ds(pl.multiple_of(y * ZA, ZA), ZA)]
@@ -194,13 +199,13 @@
         s_all[2 * i * rows_h : (2 * i + 1) * rows_h, :] = jnp.where(low, v, w).astype(BF16)
         s_all[(2 * i + 1) * rows_h : (2 * i + 2) * rows_h, :] = jnp.where(low, w, v).astype(BF16)
 
-    low = low_half((32, 128))
+    low = low_half((8, 128))
     for cc in range(2):
         t = dot(packed[cc].reshape(FX, 256), s_all[...], CONTRACT_FIRST)
-        for ah in range(4):
-            pair = jnp.where(low, t[ah * 64 : ah * 64 + 32], t[ah * 64 + 32 : ah * 64 + 64])
-            for xx in range(4):
-                t_out[cc, xx, ah] = pair[xx * 8 : xx * 8 + 8]
+        for xx in range(4):
+            for ah in range(4):
+                at_a = xx * 64 + ah * 16
+                t_out[cc, xx, ah] = jnp.where(low, t[at_a : at_a + 8], t[at_a + 8 : at_a + 16])
     got_t = [
         send(
             t_out.at[(core + dc) % 2, (x + dx) % X],
@@ -287,42 +292,44 @@
         for dx in far_x:
             got_x.append(send(spot, spot, s_x1.at[dx, dz], r_x1.at[dx, dz], at(dx=dx)))
     drain(len(got_x))
+
+    def block_of(xx):
+        rows = s_full[xx].reshape(MR, 128)
+        return rows, dot(rows, rows, CONTRACT_FIRST)
+
+    low = low_half((MR, 128))
+
+    def back(rows):
+        wide_s = rows.astype(F32)
+        turned = swap_halves(wide_s)
+        both = jnp.concatenate([jnp.where(low, wide_s, turned), jnp.where(low, turned, wide_s)], axis=0)
+        return dot(m_from[...], both.astype(BF16)).astype(BF16)
+
+    rows, big = block_of(x)
+    w_rows = back(rows)
+
     receive(got_n)
-    for i in range(0, len(got_x), len(far_x)):
-        receive(got_x[i : i + len(far_x)])
-    s_x = [s_full[i].reshape(MR, 128) for i in range(X)]
-
-    big = dot(s_x[0], s_x[0], CONTRACT_FIRST)
-    for i in range(1, X):
-        big = big + dot(s_x[i], s_x[i], CONTRACT_FIRST)
-    gram_out[...] = swap_halves(big[0:64]) + big[64:128]
-    got_g = send(gram_out, gram_in, s_g, r_g, partner)
-
-    low = low_half((MR, 128))
-    rhs = []
-    for xp in range(X // 2):
-        s0 = s_x[2 * xp].astype(F32)
-        s1 = s_x[2 * xp + 1].astype(F32)
-        rhs.append(
-            jnp.concatenate(
-                [jnp.where(low, s0, swap_halves(s1)), jnp.where(low, swap_halves(s0), s1)], axis=0
-            ).astype(BF16)
-        )
-    w = dot(m_from[...], jnp.concatenate(rhs, axis=1))
-    low = low_half((128, 128))
-    ypart = None
+    half = low_half((FC, 128))
     for dy in range(Y):
-        by_x = []
+        own = (n_in[0, dy] if dy else packed[core, y]).astype(F32)
+        other = n_in[1, dy].astype(F32)
+        spot = slice(dy * 128, dy * 128 + 128)
         for xp in range(X // 2):
-            v = w[dy * 128 : dy * 128 + 128, xp * 128 : xp * 128 + 128]
-            t = swap_halves(v)
-            by_x += [jnp.where(low, v, t), jnp.where(low, t, v)]
-        for dc in range(2):
-            tiles = [by_x[xx][a * 8 : a * 8 + 8] for a in range(dc * 8, dc * 8 + 8) for xx in range(X)]
-            w_rows = jnp.concatenate(tiles, axis=0).astype(BF16)
-            fibres = n_in[dc, dy] if dc or dy else packed[core, y]
-            term = dot(fibres, w_rows)
-            ypart = term if ypart is None else ypart + term
+            a_side = own[:, xp * 128 : xp * 128 + 128]
+            b_side = other[:, xp * 128 : xp * 128 + 128]
+            n_x[2 * xp, :, spot] = jnp.where(half, a_side, swap_halves(b_side)).astype(BF16)
+            n_x[2 * xp + 1, :, spot] = jnp.where(half, swap_halves(a_side), b_side).astype(BF16)
+    ypart = dot(n_x[x], w_rows)
+    near_x = nearest_first(X)
+    for dx in near_x:
+        receive(got_x[far_x.index(dx) :: len(far_x)])
+        xx = (x + X - dx) % X
+        rows, more = block_of(xx)
+        big = big + more
+        if dx == near_x[-1]:
+            gram_out[...] = swap_halves(big[0:64]) + big[64:128]
+            got_g = send(gram_out, gram_in, s_g, r_g, partner)
+        ypart = ypart + dot(n_x[xx], back(rows))
     ypart = jnp.where(low_half((FC // 2, 128)), ypart[0 : FC // 2], ypart[FC // 2 : FC])
     for i in range(ZL):
         for cc in range(2):
@@ -407,6 +414,8 @@
         pltpu.VMEM((FC * 8, 128), F32),
         pltpu.VMEM((2, Y, FC, 256), BF16),
         pltpu.VMEM((2, Y, FC, 256), BF16),
+        pltpu.VMEM((2, Y, FC, 256), BF16),
+        pltpu.VMEM((X, FC, Y * 128), BF16),
         pltpu.VMEM((4, 128), F32),
         pltpu.VMEM((ZC, 4, 128), F32),
         pltpu.VMEM((Y, ZC * 2, 128), BF16),

time: 57.3 us -> 59 us (1.030)
  Pallas kernels: 56.5 us -> 58.2 us
    pallas_call x1, Pallas kernels: 54.9 us -> 56.6 us  [per_device(): pl.pallas_call(functools.partial(kernel, sizes), out_shape=(jax.ShapeDtyp...]
where the time goes in v4:
time: 59 us; the launch traced here: 58.8 us
  Pallas kernels  58.2 us (99%)
  between operations  0.64 us (1%)
    pallas_call x1, Pallas kernels, per_device(): pl.pallas_call(functools.partial(kernel, sizes), out_shape=(jax.ShapeDtyp...  56.6 us
    pallas_call x1, Pallas kernels, per_device(): pl.pallas_call(functools.partial(finish, float((chips * 64) ** 0.5)), out...  1.54 us

profile of v4, /device:TPU:1, one launch (start us, length us, event | category | flops | bytes accessed | tf_op | source)
XLA Modules:
  0.0 58.8 jit_solution(4008599655042795462)
XLA Ops:
  0.6 56.6 %tucker.1 = (f32[16,128]{1,0:T(8,128)}, f32[64,128]{1,0:T(8,128)}) custom-call(bf16[4096,512]{1,0:T(8,128)(2,1)} %bitcast.3, bf16[64,512]{1,0:T(8,128)(2,1)} %bitcast.5, bf16[64,1024]{1,0:T(8,128)(2,1)} %bitcast.4, bf16[4,64]{1,0:T(4,128)(2,1)} %sketch_in.1), custom_call_target="tpu_custom_call" | custom-call | tf_op jit(solution)/shard_map/tucker/pallas_call | solution.py:459
  57.3 1.5 %finish.1 = (f32[8,64]{1,0:T(8,128)}, f32[4,64]{1,0:T(4,128)}) custom-call(f32[16,128]{1,0:T(8,128)} %get-tuple-element.4.rows, f32[64,128]{1,0:T(8,128)} %get-tuple-element.5.inverse), custom_call_target="tpu_custom_call" | custom-call | tf_op jit(solution)/shard_map/finish/pallas_call | solution.py:469

commit v5 on v4

--- a/solution.py
+++ b/solution.py
@@ -293,21 +293,6 @@
             got_x.append(send(spot, spot, s_x1.at[dx, dz], r_x1.at[dx, dz], at(dx=dx)))
     drain(len(got_x))
 
-    def block_of(xx):
-        rows = s_full[xx].reshape(MR, 128)
-        return rows, dot(rows, rows, CONTRACT_FIRST)
-
-    low = low_half((MR, 128))
-
-    def back(rows):
-        wide_s = rows.astype(F32)
-        turned = swap_halves(wide_s)
-        both = jnp.concatenate([jnp.where(low, wide_s, turned), jnp.where(low, turned, wide_s)], axis=0)
-        return dot(m_from[...], both.astype(BF16)).astype(BF16)
-
-    rows, big = block_of(x)
-    w_rows = back(rows)
-
     receive(got_n)
     half = low_half((FC, 128))
     for dy in range(Y):
@@ -319,17 +304,34 @@
             b_side = other[:, xp * 128 : xp * 128 + 128]
             n_x[2 * xp, :, spot] = jnp.where(half, a_side, swap_halves(b_side)).astype(BF16)
             n_x[2 * xp + 1, :, spot] = jnp.where(half, swap_halves(a_side), b_side).astype(BF16)
-    ypart = dot(n_x[x], w_rows)
-    near_x = nearest_first(X)
-    for dx in near_x:
-        receive(got_x[far_x.index(dx) :: len(far_x)])
-        xx = (x + X - dx) % X
-        rows, more = block_of(xx)
-        big = big + more
-        if dx == near_x[-1]:
-            gram_out[...] = swap_halves(big[0:64]) + big[64:128]
-            got_g = send(gram_out, gram_in, s_g, r_g, partner)
-        ypart = ypart + dot(n_x[xx], back(rows))
+    for i in range(0, len(got_x), len(far_x)):
+        receive(got_x[i : i + len(far_x)])
+    s_x = [s_full[i].reshape(MR, 128) for i in range(X)]
+
+    big = dot(s_x[0], s_x[0], CONTRACT_FIRST)
+    for i in range(1, X):
+        big = big + dot(s_x[i], s_x[i], CONTRACT_FIRST)
+    gram_out[...] = swap_halves(big[0:64]) + big[64:128]
+    got_g = send(gram_out, gram_in, s_g, r_g, partner)
+
+    low = low_half((MR, 128))
+    rhs = []
+    for xp in range(X // 2):
+        s0 = s_x[2 * xp].astype(F32)
+        s1 = s_x[2 * xp + 1].astype(F32)
+        rhs.append(
+            jnp.concatenate(
+                [jnp.where(low, s0, swap_halves(s1)), jnp.where(low, swap_halves(s0), s1)], axis=0
+            ).astype(BF16)
+        )
+    w_rows = dot(m_from[...], jnp.concatenate(rhs, axis=1)).astype(BF16)
+    by_x = dot(n_x[...].reshape(X * FC, Y * 128), w_rows)
+    even = by_x[0:FC, 0:128]
+    odd = by_x[FC : 2 * FC, 0:128]
+    for xp in range(1, X // 2):
+        even = even + by_x[2 * xp * FC : (2 * xp + 1) * FC, xp * 128 : xp * 128 + 128]
+        odd = odd + by_x[(2 * xp + 1) * FC : (2 * xp + 2) * FC, xp * 128 : xp * 128 + 128]
+    ypart = jnp.where(half, even + swap_halves(odd), swap_halves(even) + odd)
     ypart = jnp.where(low_half((FC // 2, 128)), ypart[0 : FC // 2], ypart[FC // 2 : FC])
     for i in range(ZL):
         for cc in range(2):

time: 59 us -> 57.5 us (0.975)
  Pallas kernels: 58.2 us -> 56.6 us
    pallas_call x1, Pallas kernels: 56.6 us -> 55.1 us  [per_device(): pl.pallas_call(functools.partial(kernel, sizes), out_shape=(jax.ShapeDtyp...]
where the time goes in v5:
time: 57.5 us; the launch traced here: 57.2 us
  Pallas kernels  56.6 us (98%)
  between operations  0.64 us (1%)
    pallas_call x1, Pallas kernels, per_device(): pl.pallas_call(functools.partial(kernel, sizes), out_shape=(jax.ShapeDtyp...  55.1 us
    pallas_call x1, Pallas kernels, per_device(): pl.pallas_call(functools.partial(finish, float((chips * 64) ** 0.5)), out...  1.54 us

profile of v5, /device:TPU:1, one launch (start us, length us, event | category | flops | bytes accessed | tf_op | source)
XLA Modules:
  0.0 57.2 jit_solution(16679718387835158727)
XLA Ops:
  0.6 55.1 %tucker.1 = (f32[16,128]{1,0:T(8,128)}, f32[64,128]{1,0:T(8,128)}) custom-call(bf16[4096,512]{1,0:T(8,128)(2,1)} %bitcast.3, bf16[64,512]{1,0:T(8,128)(2,1)} %bitcast.5, bf16[64,1024]{1,0:T(8,128)(2,1)} %bitcast.4, bf16[4,64]{1,0:T(4,128)(2,1)} %sketch_in.1), custom_call_target="tpu_custom_call" | custom-call | tf_op jit(solution)/shard_map/tucker/pallas_call | solution.py:461
  55.7 1.5 %finish.1 = (f32[8,64]{1,0:T(8,128)}, f32[4,64]{1,0:T(4,128)}) custom-call(f32[16,128]{1,0:T(8,128)} %get-tuple-element.4.rows, f32[64,128]{1,0:T(8,128)} %get-tuple-element.5.inverse), custom_call_target="tpu_custom_call" | custom-call | tf_op jit(solution)/shard_map/finish/pallas_call | solution.py:471

commit v6 on v5

--- a/solution.py
+++ b/solution.py
@@ -72,26 +72,17 @@
         row = ((y + dy) % Y) * Z + (z + dz) % Z
         return (row * 2 + (core + dc) % 2, (x + dx) % X)
 
-    waits = []
-    slow_waits = []
-
-    def send(src, dst, ssem, rsem, peer, slow=False):
+    def send(src, dst, ssem, rsem, peer):
         copy = pltpu.make_async_remote_copy(
             src_ref=src, dst_ref=dst, send_sem=ssem, recv_sem=rsem, device_id=peer, device_id_type=MESH
         )
         copy.start()
-        (slow_waits if slow else waits).append(copy)
         return copy
 
-    def receive(copies):
-        for copy in reversed(copies):
-            copy.wait_recv()
-
-    def drain(keep=0):
-        done = waits[: len(waits) - keep]
-        for copy in done:
-            copy.wait_send()
-        del waits[: len(done)]
+    def all_of(space, ssem, rsem):
+        return pltpu.make_async_remote_copy(
+            src_ref=space, dst_ref=space, send_sem=ssem, recv_sem=rsem, device_id=at(dc=1), device_id_type=MESH
+        )
 
     far_z, far_y, far_x = farthest_first(Z), farthest_first(Y), farthest_first(X)
     zc_peers = [(dc, dz) for dz in far_z + [0] for dc in range(2) if dc or dz]
@@ -150,19 +141,21 @@
 
     pl.semaphore_wait(barrier, met)
 
-    got_a = [
-        send(s_own, s_zc.at[zc], s_a.at[dc, dz], r_a.at[dc, dz], at(dz=dz, dc=dc)) for dc, dz in zc_peers
-    ]
+    for dc, dz in zc_peers:
+        send(s_own, s_zc.at[zc], s_a, r_a, at(dz=dz, dc=dc))
+    got_a = all_of(s_zc.at[pl.ds(1, ZC - 1)], s_a, r_a)
 
     lax.fori_loop(0, Y, narrow, 0)
 
-    receive(got_a)
+    got_a.wait_recv()
     half = ZC // 2
     lo = jnp.concatenate([s_zc[i] for i in range(half)], axis=0)
     hi = jnp.concatenate([s_zc[half + i] for i in range(half)], axis=0)
     rows_h = half * 4
     s_y[y] = jnp.where(low_half((rows_h, 128)), lo, hi).astype(BF16)
-    got_b = [send(s_y.at[y], s_y.at[y], s_b.at[dy], r_b.at[dy], at(dy=dy)) for dy in far_y]
+    for dy in far_y:
+        send(s_y.at[y], s_y.at[y], s_b, r_b, at(dy=dy))
+    got_b = all_of(s_y.at[pl.ds(1, Y - 1)], s_b, r_b)
 
     partner = at(dc=1)
     small[2].wait()
@@ -191,7 +184,7 @@
         keep = iota((MR, 256), 1) % 8 == rh * 4 + iota((MR, 256), 0) % 4
         m_to[rh] = jnp.where(keep, rows_a, 0.0).astype(BF16)
 
-    receive(got_b)
+    got_b.wait_recv()
     low = low_half((rows_h, 128))
     for i in range(Y):
         v = s_y[i].astype(F32)
@@ -206,39 +199,24 @@
             for ah in range(4):
                 at_a = xx * 64 + ah * 16
                 t_out[cc, xx, ah] = jnp.where(low, t[at_a : at_a + 8], t[at_a + 8 : at_a + 16])
-    got_t = [
-        send(
-            t_out.at[(core + dc) % 2, (x + dx) % X],
-            t_in.at[dc, dx],
-            s_t.at[dc, dx],
-            r_t.at[dc, dx],
-            at(dx=dx, dc=dc),
-        )
-        for dc, dx in xc_peers
-    ]
+    for dc, dx in xc_peers:
+        send(t_out.at[(core + dc) % 2, (x + dx) % X], t_in.at[dc * X + dx], s_t, r_t, at(dx=dx, dc=dc))
+    got_t = all_of(t_in.at[pl.ds(1, 2 * X - 1)], s_t, r_t)
+
     def spread_fibres(peers):
-        return [
-            send(
-                packed.at[(core + dc) % 2, (y + dy) % Y],
-                n_in.at[dc, dy],
-                s_n.at[dc, dy],
-                r_n.at[dc, dy],
-                at(dy=dy, dc=dc),
-                slow=True,
-            )
-            for dc, dy in peers
-        ]
-
-    got_n = spread_fibres([p for p in yc_peers if p[0] == 0])
+        for dc, dy in peers:
+            send(packed.at[(core + dc) % 2, (y + dy) % Y], n_in.at[dc * Y + dy], s_n, r_n, at(dy=dy, dc=dc))
+
+    spread_fibres([p for p in yc_peers if p[0] == 0])
     mine = t_out[core, x]
-    other = None
-    drain(len(got_t))
-    for (dc, dx), copy in reversed(list(zip(xc_peers, got_t))):
-        copy.wait_recv()
-        if dc == 0:
-            mine = mine + t_in[0, dx]
-        else:
-            other = t_in[1, dx] if other is None else other + t_in[1, dx]
+    for copy in (got_a, got_b):
+        copy.wait_send()
+    got_t.wait_recv()
+    for dx in range(1, X):
+        mine = mine + t_in[dx]
+    other = t_in[X]
+    for dx in range(1, X):
+        other = other + t_in[X + dx]
     u = jnp.concatenate([mine.reshape(32, 128), other.reshape(32, 128)], axis=0)
     low = low_half((64, 128))
     v = swap_halves(u)
@@ -252,11 +230,11 @@
     for i in range(Z):
         sp_out[i] = part[i * RZ : (i + 1) * RZ].astype(BF16)
 
-    got = [
-        send(sp_out.at[(z + dz) % Z], sp_in.at[dz], s_z1.at[dz], r_z1.at[dz], at(dz=dz)) for dz in far_z
-    ]
+    for dz in far_z:
+        send(sp_out.at[(z + dz) % Z], sp_in.at[dz], s_z1, r_z1, at(dz=dz))
+    got_z = all_of(sp_in.at[pl.ds(1, Z - 1)], s_z1, r_z1)
     total = sp_out[z].astype(F32)
-    drain(len(got))
+    got_t.wait_send()
 
     row = iota((128, ZA), 0)
     pick = one_hot(iota((128, ZA), 1) == z * 16 + ((core + row // 64) % 2) * 8 + (row // 8) % 8)
@@ -268,44 +246,47 @@
             keep = iota((128, MR), 0) % 8 == rh * 4 + iota((128, MR), 1) % 4
             m_from[dy * 128 : dy * 128 + 128, rh * MR : (rh + 1) * MR] = jnp.where(keep, cols_a, 0.0).astype(BF16)
 
-    for dz, copy in reversed(list(zip(far_z, got))):
-        copy.wait_recv()
+    got_z.wait_recv()
+    for dz in range(1, Z):
         total = total + sp_in[dz].astype(F32)
     z_out[...] = total.astype(BF16)
-    got = [send(z_out, z_in.at[dy], s_y1.at[dy], r_y1.at[dy], at(dy=dy)) for dy in far_y]
-    drain(len(got))
-    for dy, copy in reversed(list(zip(far_y, got))):
-        copy.wait_recv()
+    for dy in far_y:
+        send(z_out, z_in.at[dy], s_y1, r_y1, at(dy=dy))
+    got_r = all_of(z_in.at[pl.ds(1, Y - 1)], s_y1, r_y1)
+    got_z.wait_send()
+    got_r.wait_recv()
+    for dy in range(1, Y):
         total = total + z_in[dy].astype(F32)
     for i in range(Y):
         mz[i] = total[i * 4 : i * 4 + 4]
     s_full[x, z] = total.astype(BF16)
     spot = s_full.at[x, z]
-    got = {dz: send(spot, spot, s_z2.at[dz], r_z2.at[dz], at(dz=dz)) for dz in far_z}
-    got_n += spread_fibres([p for p in yc_peers if p[0] == 1])
-    got_x = []
-    drain(len(got))
+    got = {dz: send(spot, spot, s_z2, r_z2.at[dz], at(dz=dz)) for dz in far_z}
+    spread_fibres([p for p in yc_peers if p[0] == 1])
+    got_n = all_of(n_in.at[pl.ds(1, 2 * Y - 1)], s_n, r_n)
+    got_r.wait_send()
     for dz in [0] + nearest_first(Z):
         if dz:
-            receive([got[dz]])
+            got[dz].wait_recv()
         spot = s_full.at[x, (z + Z - dz) % Z]
         for dx in far_x:
-            got_x.append(send(spot, spot, s_x1.at[dx, dz], r_x1.at[dx, dz], at(dx=dx)))
-    drain(len(got_x))
-
-    receive(got_n)
+            send(spot, spot, s_x1.at[dx], r_x1.at[dx], at(dx=dx))
+    got_x = [all_of(s_full.at[(x + X - dx) % X], s_x1.at[dx], r_x1.at[dx]) for dx in nearest_first(X)]
+    all_of(sp_in.at[pl.ds(1, Z - 1)], s_z2, r_z2.at[0]).wait_send()
+
+    got_n.wait_recv()
     half = low_half((FC, 128))
     for dy in range(Y):
-        own = (n_in[0, dy] if dy else packed[core, y]).astype(F32)
-        other = n_in[1, dy].astype(F32)
+        own = (n_in[dy] if dy else packed[core, y]).astype(F32)
+        other = n_in[Y + dy].astype(F32)
         spot = slice(dy * 128, dy * 128 + 128)
         for xp in range(X // 2):
             a_side = own[:, xp * 128 : xp * 128 + 128]
             b_side = other[:, xp * 128 : xp * 128 + 128]
             n_x[2 * xp, :, spot] = jnp.where(half, a_side, swap_halves(b_side)).astype(BF16)
             n_x[2 * xp + 1, :, spot] = jnp.where(half, swap_halves(a_side), b_side).astype(BF16)
-    for i in range(0, len(got_x), len(far_x)):
-        receive(got_x[i : i + len(far_x)])
+    for copy in got_x:
+        copy.wait_recv()
     s_x = [s_full[i].reshape(MR, 128) for i in range(X)]
 
     big = dot(s_x[0], s_x[0], CONTRACT_FIRST)
@@ -336,18 +317,11 @@
     for i in range(ZL):
         for cc in range(2):
             y_out[i, cc] = ypart[i * 8 + cc * 4 : i * 8 + cc * 4 + 4]
-    got_y = [
-        send(
-            y_out.at[((z + dz) % Z) % ZL, (core + dc) % 2],
-            y_in.at[dc, dz],
-            s_y1z.at[dc, dz],
-            r_y1z.at[dc, dz],
-            at(dz=dz, dc=dc),
-        )
-        for dc, dz in zc_peers
-    ]
-
-    receive([got_g])
+    for dc, dz in zc_peers:
+        send(y_out.at[((z + dz) % Z) % ZL, (core + dc) % 2], y_in.at[dc * Z + dz], s_y1z, r_y1z, at(dz=dz, dc=dc))
+    got_y = all_of(y_in.at[pl.ds(1, 2 * Z - 1)], s_y1z, r_y1z)
+
+    got_g.wait_recv()
     g = gram_out[...] + gram_in[...]
     low = low_half((64, 128))
     g = jnp.where(low, jnp.where(iota((64, 128), 0) == iota((64, 128), 1), 1.0, 0.0), g)
@@ -389,13 +363,12 @@
     pivots = jnp.sum(diagonal, axis=1, keepdims=True)
     inverse_out[...] = elim * (1.0 / jnp.sqrt(pivots))
 
-    drain()
-    for copy in slow_waits:
+    for copy in (got_n, *got_x, got_g, got_y):
         copy.wait_send()
     acc = y_out[z % ZL, core]
-    for (dc, dz), copy in reversed(list(zip(zc_peers, got_y))):
-        copy.wait_recv()
-        acc = acc + y_in[dc, dz]
+    got_y.wait_recv()
+    for i in range(1, 2 * Z):
+        acc = acc + y_in[i]
     acc = jnp.where(z // ZL == 0, acc, swap_halves(acc))
     s_mine = mz[y]
     rows_out[...] = jnp.concatenate([s_mine, swap_halves(s_mine), acc, acc], axis=0)
@@ -416,14 +389,14 @@
         pltpu.VMEM((FC * 8, 128), F32),
         pltpu.VMEM((2, Y, FC, 256), BF16),
         pltpu.VMEM((2, Y, FC, 256), BF16),
-        pltpu.VMEM((2, Y, FC, 256), BF16),
+        pltpu.VMEM((2 * Y, FC, 256), BF16),
         pltpu.VMEM((X, FC, Y * 128), BF16),
         pltpu.VMEM((4, 128), F32),
         pltpu.VMEM((ZC, 4, 128), F32),
         pltpu.VMEM((Y, ZC * 2, 128), BF16),
         pltpu.VMEM((FX, 128), BF16),
         pltpu.VMEM((2, 4, 4, 8, 128), F32),
-        pltpu.VMEM((2, X, 4, 8, 128), F32),
+        pltpu.VMEM((2 * X, 4, 8, 128), F32),
         pltpu.VMEM((Z, RZ, 128), BF16),
         pltpu.VMEM((Z, RZ, 128), BF16),
         pltpu.VMEM((RZ, 128), BF16),
@@ -435,22 +408,22 @@
         pltpu.VMEM((64, 128), F32),
         pltpu.VMEM((64, 128), F32),
         pltpu.VMEM((ZL, 2, 4, 128), F32),
-        pltpu.VMEM((2, Z, 4, 128), F32),
+        pltpu.VMEM((2 * Z, 4, 128), F32),
         pltpu.VMEM((64, cb), BF16),
         pltpu.VMEM((chips, chips * 16), BF16),
         pltpu.VMEM((4, 64), BF16),
         dma((Y,)),
         dma((3,)),
-        dma((2, Z)), dma((2, Z)),
-        dma((Y,)), dma((Y,)),
-        dma((2, Y)), dma((2, Y)),
-        dma((2, X)), dma((2, X)),
-        dma((Z,)), dma((Z,)),
-        dma((Y,)), dma((Y,)),
-        dma((Z,)), dma((Z,)),
-        dma((X, Z)), dma((X, Z)),
-        dma, dma,
-        dma((2, Z)), dma((2, Z)),
+        dma, dma,
+        dma, dma,
+        dma, dma,
+        dma, dma,
+        dma, dma,
+        dma, dma,
+        dma, dma((Z,)),
+        dma((X,)), dma((X,)),
+        dma, dma,
+        dma, dma,
     ]
 
 

time: 57.5 us -> 55.6 us (0.967)
  Pallas kernels: 56.6 us -> 54.7 us
    pallas_call x1, Pallas kernels: 55.1 us -> 53.2 us  [per_device(): pl.pallas_call(functools.partial(kernel, sizes), out_shape=(jax.ShapeDtyp...]
where the time goes in v6:
time: 55.6 us; the launch traced here: 55.4 us
  Pallas kernels  54.7 us (98%)
  between operations  0.64 us (1%)
    pallas_call x1, Pallas kernels, per_device(): pl.pallas_call(functools.partial(kernel, sizes), out_shape=(jax.ShapeDtyp...  53.2 us
    pallas_call x1, Pallas kernels, per_device(): pl.pallas_call(functools.partial(finish, float((chips * 64) ** 0.5)), out...  1.54 us

profile of v6, /device:TPU:1, one launch (start us, length us, event | category | flops | bytes accessed | tf_op | source)
XLA Modules:
  0.0 55.4 jit_solution(1859973158572240537)
XLA Ops:
  0.6 53.2 %tucker.1 = (f32[16,128]{1,0:T(8,128)}, f32[64,128]{1,0:T(8,128)}) custom-call(bf16[4096,512]{1,0:T(8,128)(2,1)} %bitcast.3, bf16[64,512]{1,0:T(8,128)(2,1)} %bitcast.5, bf16[64,1024]{1,0:T(8,128)(2,1)} %bitcast.4, bf16[4,64]{1,0:T(4,128)(2,1)} %sketch_in.1), custom_call_target="tpu_custom_call" | custom-call | tf_op jit(solution)/shard_map/tucker/pallas_call | solution.py:434
  53.8 1.5 %finish.1 = (f32[8,64]{1,0:T(8,128)}, f32[4,64]{1,0:T(4,128)}) custom-call(f32[16,128]{1,0:T(8,128)} %get-tuple-element.4.rows, f32[64,128]{1,0:T(8,128)} %get-tuple-element.5.inverse), custom_call_target="tpu_custom_call" | custom-call | tf_op jit(solution)/shard_map/finish/pallas_call | solution.py:444

commit v7 on v6

--- a/solution.py
+++ b/solution.py
@@ -42,13 +42,12 @@
     return sorted(range(1, n), key=lambda d: min(d, n - d))
 
 
-def finish(scale, rows, inverse, transfer, coefficients):
-    out = dot(rows[:, 0:64], inverse[:, 0:64], CONTRACT_LAST, lax.Precision.HIGHEST)
-    transfer[...] = out[0:8] * scale
-    coefficients[...] = out[8:12]
-
-
-def kernel(sizes, blocks, basis_b_in, basis_a_in, sketch_in, rows_out, inverse_out, *scratch):
+def finish(rows, transfer, coefficients):
+    transfer[...] = rows[0:8, 0:64]
+    coefficients[...] = rows[8:12, 0:64]
+
+
+def kernel(sizes, blocks, basis_b_in, basis_a_in, sketch_in, rows_out, *scratch):
     X, Y, Z = sizes
     ZC = Z * 2
     ZL = Z // 2
@@ -361,7 +360,7 @@
     elim = jnp.concatenate(tiles, axis=0)
     diagonal = jnp.where(iota((64, 128), 1) == iota((64, 128), 0) + 64, elim, 0.0)
     pivots = jnp.sum(diagonal, axis=1, keepdims=True)
-    inverse_out[...] = elim * (1.0 / jnp.sqrt(pivots))
+    inverse = elim * (1.0 / jnp.sqrt(pivots))
 
     for copy in (got_n, *got_x, got_g, got_y):
         copy.wait_send()
@@ -371,7 +370,10 @@
         acc = acc + y_in[i]
     acc = jnp.where(z // ZL == 0, acc, swap_halves(acc))
     s_mine = mz[y]
-    rows_out[...] = jnp.concatenate([s_mine, swap_halves(s_mine), acc, acc], axis=0)
+    rows = jnp.concatenate([s_mine, swap_halves(s_mine), acc, acc], axis=0)
+    out = dot(rows[:, 0:64], inverse[:, 0:64], CONTRACT_LAST, lax.Precision.HIGHEST)
+    rows_out[0:8, 0:64] = out[0:8] * float((chips * 64) ** 0.5)
+    rows_out[8:16, 0:64] = out[8:16]
 
 
 def scratch_for(sizes, cb):
@@ -431,23 +433,22 @@
     fibres, own_a, cb = blocks.shape
     vmem = pl.BlockSpec(memory_space=pltpu.VMEM)
     anywhere = pl.BlockSpec(memory_space=pl.ANY)
-    rows, inverse = pl.pallas_call(
+    rows = pl.pallas_call(
         functools.partial(kernel, sizes),
-        out_shape=(jax.ShapeDtypeStruct((16, 128), F32), jax.ShapeDtypeStruct((64, 128), F32)),
+        out_shape=jax.ShapeDtypeStruct((16, 128), F32),
         in_specs=[anywhere] * 4,
-        out_specs=(vmem, vmem),
+        out_specs=vmem,
         scratch_shapes=scratch_for(sizes, cb),
         compiler_params=pltpu.CompilerParams(collective_id=0, has_side_effects=True),
         name="tucker",
     )(blocks.reshape(fibres * own_a, cb), basis_b.T, basis_a.T, sketch)
-    chips = sizes[1] * sizes[2]
     return pl.pallas_call(
-        functools.partial(finish, float((chips * 64) ** 0.5)),
+        finish,
         out_shape=(jax.ShapeDtypeStruct((8, 64), F32), jax.ShapeDtypeStruct((4, 64), F32)),
-        in_specs=[vmem, vmem],
+        in_specs=[vmem],
         out_specs=(vmem, vmem),
         name="finish",
-    )(rows, inverse)
+    )(rows)
 
 
 def solution(mesh):

time: 55.6 us -> 55.6 us (level)
  no operation moved by 1% of the time
where the time goes in v7:
time: 55.6 us; the launch traced here: 55.4 us
  Pallas kernels  54.8 us (99%)
  between operations  0.64 us (1%)
    pallas_call x1, Pallas kernels, per_device(): pl.pallas_call(functools.partial(kernel, sizes), out_shape=jax.ShapeDtype...  53.5 us
    pallas_call x1, Pallas kernels, per_device(): pl.pallas_call(finish, out_shape=(jax.ShapeDtypeStruct((8, 64), F32), jax...  1.29 us

profile of v7, /device:TPU:1, one launch (start us, length us, event | category | flops | bytes accessed | tf_op | source)
XLA Modules:
  0.0 55.4 jit_solution(4729375098987572823)
XLA Ops:
  0.6 53.5 %tucker.1.rows = f32[16,128]{1,0:T(8,128)} custom-call(bf16[4096,512]{1,0:T(8,128)(2,1)} %bitcast.3, bf16[64,512]{1,0:T(8,128)(2,1)} %bitcast.5, bf16[64,1024]{1,0:T(8,128)(2,1)} %bitcast.4, bf16[4,64]{1,0:T(4,128)(2,1)} %sketch_in.1), custom_call_target="tpu_custom_call" | custom-call | tf_op jit(solution)/shard_map/tucker/pallas_call | solution.py:436
  54.2 1.3 %finish.1 = (f32[8,64]{1,0:T(8,128)}, f32[4,64]{1,0:T(4,128)}) custom-call(f32[16,128]{1,0:T(8,128)} %tucker.1.rows), custom_call_target="tpu_custom_call" | custom-call | tf_op jit(solution)/shard_map/finish/pallas_call | solution.py:445
